TPU v7x, 32 devices: a whole 2x2x4 slice. The times are simulated.
32 devices in a mesh: dp: 8 (over z, y), tensor: 4 (over x, core).
Axes of the slice: x: 2, y: 2, z: 4, core: 2. Of those that a mesh axis runs over, the one named last changes fastest.
Arguments:
- frames: bfloat16 [16, 256, 1024], P('dp', 'tensor'), may hold values from -6 to 6
- lengths: int32 [16], P('dp'), may hold values from 128 to 256, as said below
- span_starts: int32 [16, 32], P('dp'), may hold values from 0 to 256, as said below
- mask_vector: bfloat16 [1024], P(('dp', 'tensor')), may hold values from -6 to 6
- ffn1_gain: float32 [1024], P(('dp', 'tensor')), may hold values from 0.5 to 1.5
- ffn1_up: bfloat16 [1024, 4096], P(None, 'tensor'), may hold values from -0.1875 to 0.1875
- ffn1_down: bfloat16 [4096, 1024], P('tensor'), may hold values from -0.1875 to 0.1875
- attn_gain: float32 [1024], P(('dp', 'tensor')), may hold values from 0.5 to 1.5
- query_weight: bfloat16 [1024, 1024], P(None, 'tensor'), may hold values from -0.1875 to 0.1875
- key_weight: bfloat16 [1024, 1024], P(None, 'tensor'), may hold values from -0.1875 to 0.1875
- value_weight: bfloat16 [1024, 1024], P(None, 'tensor'), may hold values from -0.1875 to 0.1875
- output_weight: bfloat16 [1024, 1024], P('tensor'), may hold values from -1.5 to 1.5
- rel_slope: float32 [8], P('tensor'), may hold values from -2 to 2
- conv_gain: float32 [1024], P(('dp', 'tensor')), may hold values from 0.5 to 1.5
- conv_up: bfloat16 [1024, 2, 1024], P('dp', None, 'tensor'), may hold values from -0.1875 to 0.1875
- conv_depth: float32 [5, 1024], P(None, 'tensor'), may hold values from -2.5 to 2.5
- bn_scale: float32 [1024], P('tensor'), may hold values from 0.5 to 1.5
- bn_shift: float32 [1024], P('tensor'), may hold values from -1 to 1
- conv_down: bfloat16 [1024, 1024], P('tensor', 'dp'), may hold values from -0.25 to 0.25
- ffn2_gain: float32 [1024], P(('dp', 'tensor')), may hold values from 0.5 to 1.5
- ffn2_up: bfloat16 [1024, 4096], P(None, 'tensor'), may hold values from -0.1875 to 0.1875
- ffn2_down: bfloat16 [4096, 1024], P('tensor'), may hold values from -0.1875 to 0.1875
- final_gain: float32 [1024], P(('dp', 'tensor')), may hold values from 0.5 to 1.5
- cotangent: bfloat16 [16, 256, 1024], P('dp', 'tensor'), may hold values from -6 to 6
Outputs:
- layer_out: bfloat16 [16, 256, 1024], P('dp', 'tensor')
- frames_grad: float32 [16, 256, 1024], P('dp', 'tensor')
- mask_vector_grad: float32 [1024], P(('dp', 'tensor'))
- ffn1_gain_grad: float32 [1024], P(('dp', 'tensor'))
- ffn1_up_grad: float32 [1024, 4096], P('dp', 'tensor')
- ffn1_down_grad: float32 [4096, 1024], P('tensor', 'dp')
- attn_gain_grad: float32 [1024], P(('dp', 'tensor'))
- query_weight_grad: float32 [1024, 1024], P('dp', 'tensor')
- key_weight_grad: float32 [1024, 1024], P('dp', 'tensor')
- value_weight_grad: float32 [1024, 1024], P('dp', 'tensor')
- output_weight_grad: float32 [1024, 1024], P('tensor', 'dp')
- rel_slope_grad: float32 [8], P('tensor')
- conv_gain_grad: float32 [1024], P(('dp', 'tensor'))
- conv_up_grad: float32 [1024, 2, 1024], P('dp', None, 'tensor')
- conv_depth_grad: float32 [5, 1024], P(None, 'tensor')
- bn_scale_grad: float32 [1024], P('tensor')
- bn_shift_grad: float32 [1024], P('tensor')
- conv_down_grad: float32 [1024, 1024], P('tensor', 'dp')
- ffn2_gain_grad: float32 [1024], P(('dp', 'tensor'))
- ffn2_up_grad: float32 [1024, 4096], P('dp', 'tensor')
- ffn2_down_grad: float32 [4096, 1024], P('tensor', 'dp')
- final_gain_grad: float32 [1024], P(('dp', 'tensor'))
Inputs may be any that keep to these rules, and one draw needn't show every extreme that they name: `lengths`: the valid frames of an utterance are its first ones; in every draw some utterance has 256 valid frames and some has 128. `span_starts`: A start of 256 marks an unused span slot; used slots come first, and each utterance uses from 8 to 31 of them. Spans may intersect one another and the padding.
All inputs are finite; a program needn't handle non-finite values.
Results may differ from a plain program's by a relative error of at most 0.04.
Values may be sent and summed in bfloat16 or wider, within the bound.
No kernel may reach another device: no remote copies, remote signals or barrier semaphores. Data moves between devices by JAX's collectives and lax.ppermute only.
A program may use at most 128 MiB of HBM per device.

v0:
```python
import functools

import jax
import jax.numpy as jnp
from jax import lax
from jax.experimental import pallas as pl
from jax.experimental.pallas import tpu as pltpu
from jax.sharding import PartitionSpec as P

DH = 128
KW = 5
SPAN = 10
REACH = 128
EPSILON = 1e-05
MASKED_SCORE = -1000000000.0
BF = jnp.bfloat16
F32 = jnp.float32
STEP = 32
TILE = 256
EDGE = 8
MIB = 1024 * 1024
COST = 30_000_000

VMEM_SPEC = pl.BlockSpec(memory_space=pltpu.VMEM)
SMEM_SPEC = pl.BlockSpec(memory_space=pltpu.SMEM)


def product(left, right):
    return jnp.dot(left, right, preferred_element_type=F32)


def inner_rows(left, right):
    return lax.dot_general(left, right, (((0,), (0,)), ((), ())), preferred_element_type=F32)


def times_back(left, right):
    return lax.dot_general(left, right, (((1,), (1,)), ((), ())), preferred_element_type=F32)


def sigmoid(values):
    return 0.5 * jnp.tanh(0.5 * values) + 0.5


def norm_unit(values):
    centre = jnp.mean(values, axis=-1, keepdims=True)
    centred = values - centre
    inverse = lax.rsqrt(jnp.mean(centred * centred, axis=-1, keepdims=True) + EPSILON)
    return centred * inverse, inverse


def norm_back(grad_out, unit_rows, inverse, norm_gain):
    grad_unit = grad_out * norm_gain
    first_mean = jnp.mean(grad_unit, axis=-1, keepdims=True)
    second_mean = jnp.mean(grad_unit * unit_rows, axis=-1, keepdims=True)
    return (
        inverse * (grad_unit - first_mean - unit_rows * second_mean),
        jnp.sum(grad_out * unit_rows, axis=0, keepdims=True),
    )


def silu_slope(values):
    gate_value = sigmoid(values)
    return gate_value * (1.0 + values * (1.0 - gate_value))


def over_rows(count, body, init=0, step=STEP):
    def one(index, carry):
        return body(pl.ds(pl.multiple_of(index * step, step), step), index * step, carry)

    return lax.fori_loop(0, count // step, one, init, unroll=4)


def row_iota(first, rows, columns):
    return first + lax.broadcasted_iota(jnp.int32, (rows, columns), 0)


def mask_col(starts_ref, first, rows, length):
    starts = starts_ref[...]
    at = row_iota(first, rows, starts.shape[1])
    hit = (starts <= at) & (at < starts + SPAN) & (at < length)
    return jnp.max(jnp.where(hit, 1.0, 0.0), axis=1, keepdims=True)


def valid_col(first, rows, columns, length):
    return jnp.where(row_iota(first, rows, columns) < length, 1.0, 0.0)


def masked_rows(frame_rows, mask, mask_row):
    return jnp.where(
        jnp.broadcast_to(mask, frame_rows.shape) > 0.5, mask_row, frame_rows.astype(F32)
    )


def pair_sum(mine, theirs, rows):
    return mine[rows, :].astype(F32) + theirs[rows, :].astype(F32)


class Late:
    def __init__(self, source, held, semaphore):
        self.copy = pltpu.make_async_copy(source, held, semaphore)
        self.copy.start()
        self.held, self.shape, self.dtype, self.waited = held, held.shape, held.dtype, False

    def arrive(self):
        if not self.waited:
            self.copy.wait()
            self.waited = True

    def __getitem__(self, index):
        assert self.waited
        return self.held[index]


class Leaving:
    def __init__(self, target, held, semaphore):
        self.copy = pltpu.make_async_copy(held, target, semaphore)
        self.held, self.shape, self.dtype, self.started = held, held.shape, held.dtype, False

    def leave(self):
        if not self.started:
            self.copy.start()
            self.started = True

    def finish(self):
        self.leave()
        self.copy.wait()

    def __getitem__(self, index):
        return self.held[index]

    def __setitem__(self, index, value):
        assert not self.started
        self.held[index] = value


def arrive(*refs):
    for ref in refs:
        if isinstance(ref, Late):
            ref.arrive()


def leave(*refs):
    for ref in refs:
        if isinstance(ref, Leaving):
            ref.leave()


def columns(index, size=TILE):
    return slice(index * size, (index + 1) * size)


def ffn_up(branch, ups, hidden, active_own, active_cross):
    normed = branch[...]
    for shard, weight in enumerate(ups):
        arrive(weight)
        tiles = weight.shape[1] // TILE
        for index in range(tiles):
            at = columns(index)
            values = product(normed, weight[:, at])
            hidden[:, columns(index + shard * tiles)] = values
            (active_own, active_cross)[shard][:, at] = (values * sigmoid(values)).astype(BF)


def ffn_down(active_own, active_cross, downs, part):
    width = downs[0].shape[1]
    own, cross = active_own[...], active_cross[...]
    arrive(*downs)
    for index in range(width // TILE):
        at = columns(index)
        part[:, at] = (product(own, downs[0][:, at]) + product(cross, downs[1][:, at])).astype(BF)


def ffn_grad_hidden(branch, downs, hidden, grad_own, grad_cross):
    grad_branch = branch[...]
    for shard, weight in enumerate(downs):
        arrive(weight)
        tiles = weight.shape[0] // TILE
        for index in range(tiles):
            at = columns(index)
            slope = silu_slope(hidden[:, columns(index + shard * tiles)])
            grad = (times_back(grad_branch, weight[at, :]) * slope).astype(BF)
            (grad_own, grad_cross)[shard][:, at] = grad


def ffn_grad_input(grad_own, grad_cross, ups, store):
    own, cross = grad_own[...], grad_cross[...]
    arrive(*ups)
    for index in range(ups[0].shape[0] // TILE):
        at = columns(index)
        store(at, times_back(own, ups[0][at, :]) + times_back(cross, ups[1][at, :]))


def k_pick(info, block, across_block, sent):
    core = info[0]
    sent[0] = block[pl.ds(1 - core, 1)][0]
    sent[1] = across_block[pl.ds(1 - core, 1)][0]


def place_rows(info, block, across_block, arrived, whole):
    core, high = info[0], info[1]
    rows = block.shape[1]
    places = (
        (2 * high + core, block[pl.ds(core, 1)][0]),
        (2 * (1 - high) + core, across_block[pl.ds(core, 1)][0]),
        (2 * high + 1 - core, arrived[0]),
        (2 * (1 - high) + 1 - core, arrived[1]),
    )
    for place, value in places:
        whole[pl.ds(pl.multiple_of(place * rows, rows), rows), :] = value


def k_ffn_one(
    info, starts, block, across_block, arrived, small, up_o, up_t, down_o, down_t,
    frames, branch, active_cross, active_own, hidden, part, whole,
):
    length = info[2]
    rows, width = whole.shape
    place_rows(info, block, across_block, arrived, whole)
    frames[...] = whole[...]

    def normalise(at, first, carry):
        mask = mask_col(starts, first, STEP, length)
        unit_rows, _ = norm_unit(masked_rows(whole[at, :], mask, small[0:1, :]))
        branch[at, :] = (unit_rows * small[1:2, :]).astype(BF)
        return carry

    over_rows(rows, normalise)
    ffn_up(branch, (up_o, up_t), hidden, active_own, active_cross)
    ffn_down(active_own, active_cross, (down_o, down_t), part)


def k_attn(
    info, starts, slopes, mine, theirs, frames, small, qkv_o, qkv_t, out_o, out_t,
    stream, branch, context_cross, context_own, qkv, weights, part,
):
    length = info[2]
    rows, width = frames.shape
    arrive(frames)

    def normalise(at, first, carry):
        mask = mask_col(starts, first, STEP, length)
        inputs = masked_rows(frames[at, :], mask, small[0:1, :])
        values = inputs + 0.5 * pair_sum(mine, theirs, at)
        stream[at, :] = values
        unit_rows, _ = norm_unit(values)
        branch[at, :] = (unit_rows * small[2:3, :]).astype(BF)
        return carry

    over_rows(rows, normalise)
    normed = branch[...]
    third = qkv_o.shape[1] // 3
    for shard, weight in enumerate((qkv_o, qkv_t)):
        arrive(weight)
        for index in range(3):
            at = columns(index, third)
            qkv[:, columns(3 * shard + index, third)] = product(normed, weight[:, at]).astype(BF)
    heads = third // DH
    span = rows // 2
    for shard in range(2):
        base = 3 * third * shard
        for head in range(heads):
            place = shard * heads + head
            key = qkv[:, base + third + head * DH : base + third + (head + 1) * DH]
            value = qkv[:, base + 2 * third + head * DH : base + 2 * third + (head + 1) * DH]
            for part_index in range(2):
                at = columns(part_index, span)
                query = qkv[at, base + head * DH : base + (head + 1) * DH]
                scores = times_back(query, key) * DH ** (-0.5)
                key_place = lax.broadcasted_iota(jnp.int32, (span, rows), 1)
                away = key_place - row_iota(part_index * span, span, rows)
                relative = jnp.clip(away, -REACH, REACH).astype(F32) * (1.0 / REACH)
                scores = scores + slopes[place] * relative
                scores = jnp.where(key_place < length, scores, MASKED_SCORE)
                raised = jnp.exp(scores - jnp.max(scores, axis=-1, keepdims=True))
                soft = raised * (1.0 / jnp.sum(raised, axis=-1, keepdims=True))
                weights[place, at, :] = soft
                context = product(soft.astype(BF), value).astype(BF)
                if shard == 0:
                    context_own[at, columns(head, DH)] = context
                else:
                    context_cross[at, columns(head, DH)] = context
    arrive(out_o, out_t)
    own = context_own[...]
    other = context_cross[...]
    for index in range(width // TILE):
        at = columns(index)
        part[:, at] = (product(own, out_o[:, at]) + product(other, out_t[:, at])).astype(BF)


def k_conv_front(
    info, mine, theirs, stream_in, small, params, conv_o, conv_t,
    stream, normed, value, gate, padded, convolved, stats,
):
    length = info[2]
    rows, width = stream_in.shape
    channels = params.shape[1] // 2
    arrive(stream_in)

    def normalise(at, first, carry):
        values = stream_in[at, :] + pair_sum(mine, theirs, at)
        stream[at, :] = values
        unit_rows, _ = norm_unit(values)
        normed[at, :] = (unit_rows * small[3:4, :]).astype(BF)
        return carry

    over_rows(rows, normalise)
    normed_rows = normed[...]
    edge = jnp.zeros((EDGE, 2 * channels), F32)
    padded[:EDGE, :] = edge
    padded[EDGE + rows :, :] = edge
    for shard, weight in enumerate((conv_o, conv_t)):
        arrive(weight)
        at = columns(shard, channels)
        value_rows = product(normed_rows, weight[:, :channels])
        value[:, at] = value_rows
        gate_rows = sigmoid(product(normed_rows, weight[:, channels : 2 * channels]))
        gate[:, at] = gate_rows
        padded[EDGE : EDGE + rows, at] = (
            value_rows * gate_rows * valid_col(0, rows, channels, length)
        )
    count = length.astype(F32)
    for tile in range(2 * channels // DH):
        at = columns(tile, DH)
        total = params[0:1, at] * padded[EDGE - 2 : EDGE - 2 + rows, at]
        for offset in range(1, KW):
            begin = EDGE - 2 + offset
            total = total + params[offset : offset + 1, at] * padded[begin : begin + rows, at]
        convolved[:, at] = total
        keep = valid_col(0, rows, DH, length)
        mean = jnp.sum(total * keep, axis=0, keepdims=True) / count
        centred = (total - mean) * keep
        stats[0:1, at] = jnp.full((1, DH), count, F32)
        stats[1:2, at] = mean
        stats[2:3, at] = jnp.sum(centred * centred, axis=0, keepdims=True)
        stats[3:8, at] = jnp.zeros((5, DH), F32)


def merged(mine, theirs):
    total = mine[0:1, :] + theirs[0:1, :]
    apart = mine[1:2, :] - theirs[1:2, :]
    mean = (mine[0:1, :] * mine[1:2, :] + theirs[0:1, :] * theirs[1:2, :]) / total
    share = mine[0:1, :] * theirs[0:1, :] / total
    spread = mine[2:3, :] + theirs[2:3, :] + apart * apart * share
    return total, mean, spread


def k_merge(mine, theirs, result):
    total, mean, spread = merged(mine, theirs)
    result[0:1, :] = total
    result[1:2, :] = mean
    result[2:3, :] = spread
    result[3:8, :] = jnp.zeros((5, result.shape[1]), F32)


def k_add(mine, theirs, result):
    result[...] = mine[...] + theirs[...]


def shaped_rows(convolved, stats, params, at):
    unit_bn = (convolved[at, :] - stats[1:2, :]) * stats[2:3, :]
    return unit_bn, unit_bn * params[5:6, :] + params[6:7, :]


def k_conv_rear(
    mine, theirs, convolved, params, normed, conv_o, conv_t,
    stats, active_own, active_cross, part,
):
    rows, width = normed.shape
    channels = params.shape[1] // 2
    total, mean, spread = merged(mine, theirs)
    arrive(convolved)
    stats[0:1, :] = total
    stats[1:2, :] = mean
    stats[2:3, :] = lax.rsqrt(spread / total + EPSILON)
    stats[3:8, :] = jnp.zeros((5, stats.shape[1]), F32)

    def activate(at, first, carry):
        _, shaped = shaped_rows(convolved, stats, params, at)
        active = (shaped * sigmoid(shaped)).astype(BF)
        active_own[at, :] = active[:, :channels]
        active_cross[at, :] = active[:, channels:]
        return carry

    over_rows(rows, activate)
    arrive(conv_o, conv_t)
    own = active_own[...]
    other = active_cross[...]
    for index in range(width // TILE):
        at = columns(index)
        part[:, at] = (
            times_back(own, conv_o[at, 2 * channels :])
            + times_back(other, conv_t[at, 2 * channels :])
        ).astype(BF)


def k_ffn_two(
    mine, theirs, stream_in, small, up_o, up_t, down_o, down_t,
    stream, branch, active_cross, active_own, hidden, part,
):
    rows, width = stream_in.shape
    arrive(stream_in)

    def normalise(at, first, carry):
        values = stream_in[at, :] + pair_sum(mine, theirs, at)
        stream[at, :] = values
        unit_rows, _ = norm_unit(values)
        branch[at, :] = (unit_rows * small[4:5, :]).astype(BF)
        return carry

    over_rows(rows, normalise)
    ffn_up(branch, (up_o, up_t), hidden, active_own, active_cross)
    ffn_down(active_own, active_cross, (down_o, down_t), part)


def split_blocks(info, rows, source, own, sent):
    core, high = info[0], info[1]
    own[...] = source[pl.ds((2 * high + core) * rows, rows), :]
    sent[...] = source[pl.ds((2 * high + 1 - core) * rows, rows), :]


def k_ffn_two_back(
    info, mine, theirs, stream, small, block, across_block, arrived, hidden,
    up_o, up_t, down_o, down_t,
    out_own, out_sent, grad_four, gain_sum, branch, grad_cross, grad_own, part, out_rows, grads,
):
    rows, width = stream.shape
    arrive(block, across_block, arrived)
    place_rows(info, block, across_block, arrived, grads)
    arrive(stream)

    def pass_back(at, first, carry):
        values = stream[at, :] + 0.5 * pair_sum(mine, theirs, at)
        unit_rows, inverse = norm_unit(values)
        out_rows[at, :] = (unit_rows * small[5:6, :]).astype(BF)
        grad, fresh = norm_back(grads[at, :].astype(F32), unit_rows, inverse, small[5:6, :])
        grad_four[at, :] = grad
        branch[at, :] = (0.5 * grad).astype(BF)
        return carry + fresh

    gain_sum[...] = over_rows(rows, pass_back, jnp.zeros((1, width), F32))
    split_blocks(info, rows // 4, out_rows, out_own, out_sent)
    ffn_grad_hidden(branch, (down_o, down_t), hidden, grad_own, grad_cross)

    def store(at, values):
        part[:, at] = values.astype(BF)

    ffn_grad_input(grad_own, grad_cross, (up_o, up_t), store)


def k_conv_back_front(
    mine, theirs, stream, small, grad_in, convolved, stats, params, conv_o, conv_t,
    grad_out, gain_sum, branch, grad_shaped, sums,
):
    rows, width = stream.shape
    channels = params.shape[1] // 2
    arrive(stream)

    def pass_back(at, first, carry):
        unit_rows, inverse = norm_unit(stream[at, :])
        grad, fresh = norm_back(pair_sum(mine, theirs, at), unit_rows, inverse, small[4:5, :])
        grad = grad_in[at, :] + grad
        grad_out[at, :] = grad
        branch[at, :] = grad.astype(BF)
        return carry + fresh

    gain_sum[...] = over_rows(rows, pass_back, jnp.zeros((1, width), F32))
    branch_rows = branch[...]
    arrive(convolved)
    for shard, weight in enumerate((conv_o, conv_t)):
        arrive(weight)
        grad_shaped[:, columns(shard, channels)] = product(branch_rows, weight[:, 2 * channels :])

    def slope(at, first, carry):
        unit_bn, shaped = shaped_rows(convolved, stats, params, at)
        grad = grad_shaped[at, :] * silu_slope(shaped)
        grad_shaped[at, :] = grad
        return (
            carry[0] + jnp.sum(grad, axis=0, keepdims=True),
            carry[1] + jnp.sum(grad * unit_bn, axis=0, keepdims=True),
        )

    zero = jnp.zeros((1, 2 * channels), F32)
    shift_sum, scale_sum = over_rows(rows, slope, (zero, zero))
    sums[0:1, :] = shift_sum
    sums[1:2, :] = scale_sum
    sums[2:8, :] = jnp.zeros((6, 2 * channels), F32)


def k_conv_back_rear(
    info, sums_mine, sums_theirs, grad_shaped, convolved, stats, params, padded, value, gate, branch,
    conv_o, conv_t,
    small_sums, mixed_own, mixed_cross, part, grad_padded,
):
    length = info[2]
    rows, width = branch.shape
    channels = params.shape[1] // 2
    sums = sums_mine[0:2, :] + sums_theirs[0:2, :]
    small_sums[5:6, :] = sums[0:1, :]
    small_sums[6:7, :] = sums[1:2, :]
    small_sums[7:8, :] = jnp.zeros((1, 2 * channels), F32)
    edge = jnp.zeros((EDGE, 2 * channels), F32)
    grad_padded[:EDGE, :] = edge
    grad_padded[EDGE + rows :, :] = edge
    arrive(convolved)
    count, bn_inverse, scale_row = stats[0:1, :], stats[2:3, :], params[5:6, :]
    grad_centre = -bn_inverse * scale_row * sums[0:1, :]
    grad_spread = -bn_inverse * bn_inverse * scale_row * sums[1:2, :]

    def spread(at, first, carry):
        centred = convolved[at, :] - stats[1:2, :]
        keep = valid_col(first, STEP, 2 * channels, length)
        grad = grad_shaped[at, :] * scale_row * bn_inverse + keep * (
            grad_centre + grad_spread * centred
        ) * (1.0 / count)
        grad_padded[pl.ds(pl.multiple_of(EDGE + first, EDGE), STEP), :] = grad
        return carry

    over_rows(rows, spread)
    arrive(padded, gate, value)
    for tile in range(2 * channels // DH):
        at = columns(tile, DH)
        grad = grad_padded[EDGE : EDGE + rows, at]
        back = None
        for offset in range(KW):
            begin = EDGE + 2 - offset
            term = params[offset : offset + 1, at] * grad_padded[begin : begin + rows, at]
            back = term if back is None else back + term
            begin = EDGE - 2 + offset
            small_sums[offset : offset + 1, at] = jnp.sum(
                grad * padded[begin : begin + rows, at], axis=0, keepdims=True
            )
        back = back * valid_col(0, rows, DH, length)
        gate_rows = gate[:, at]
        first_grad = (back * gate_rows).astype(BF)
        second_grad = (back * value[:, at] * gate_rows * (1.0 - gate_rows)).astype(BF)
        inner = (tile * DH) % channels
        if tile * DH < channels:
            mixed_own[:, inner : inner + DH] = first_grad
            mixed_own[:, channels + inner : channels + inner + DH] = second_grad
        else:
            mixed_cross[:, inner : inner + DH] = first_grad
            mixed_cross[:, channels + inner : channels + inner + DH] = second_grad
    arrive(conv_o, conv_t)
    own = mixed_own[...]
    other = mixed_cross[...]
    for index in range(width // TILE):
        at = columns(index)
        part[:, at] = (
            times_back(own, conv_o[at, : 2 * channels])
            + times_back(other, conv_t[at, : 2 * channels])
        ).astype(BF)


def k_attn_back(
    mine, theirs, stream, small, grad_in, sums_in, qkv, weights, qkv_o, qkv_t, out_o, out_t,
    grad_out, gain_sum, branch, three_cross, three_own, small_sums, part, grad_context,
):
    rows, width = stream.shape
    arrive(stream)
    third = qkv_o.shape[1] // 3
    heads = third // DH

    def pass_back(at, first, carry):
        unit_rows, inverse = norm_unit(stream[at, :])
        grad, fresh = norm_back(pair_sum(mine, theirs, at), unit_rows, inverse, small[3:4, :])
        grad = grad_in[at, :] + grad
        grad_out[at, :] = grad
        branch[at, :] = grad.astype(BF)
        return carry + fresh

    gain_sum[...] = over_rows(rows, pass_back, jnp.zeros((1, width), F32))
    branch_rows = branch[...]
    for shard, weight in enumerate((out_o, out_t)):
        arrive(weight)
        grad_context[:, columns(shard, third)] = times_back(branch_rows, weight[...]).astype(BF)
    away = lax.broadcasted_iota(jnp.int32, (rows, rows), 1) - row_iota(0, rows, rows)
    relative = jnp.clip(away, -REACH, REACH).astype(F32) * (1.0 / REACH)
    scale = DH ** (-0.5)
    arrive(qkv, weights)
    lanes = small_sums.shape[1]
    lane = lax.broadcasted_iota(jnp.int32, (1, lanes), 1)
    slope_row = jnp.zeros((1, lanes), F32)
    for shard in range(2):
        base = 3 * third * shard
        for head in range(heads):
            place = shard * heads + head
            query = qkv[:, base + head * DH : base + (head + 1) * DH]
            key = qkv[:, base + third + head * DH : base + third + (head + 1) * DH]
            value = qkv[:, base + 2 * third + head * DH : base + 2 * third + (head + 1) * DH]
            grad_head = grad_context[:, place * DH : (place + 1) * DH]
            soft = weights[place]
            grad_soft = times_back(grad_head, value)
            grad_value = inner_rows(soft.astype(BF), grad_head)
            dots = jnp.sum(soft * grad_soft, axis=-1, keepdims=True)
            grad_scores = (soft * (grad_soft - dots)).astype(BF)
            tilted = jnp.sum(grad_scores.astype(F32) * relative, axis=0, keepdims=True)
            slope = jnp.broadcast_to(jnp.sum(tilted, axis=1, keepdims=True), (1, lanes))
            slope_row = jnp.where(lane == shard * (lanes // 2) + head, slope, slope_row)
            grads = (
                product(grad_scores, key) * scale,
                inner_rows(grad_scores, query) * scale,
                grad_value,
            )
            for index, grad in enumerate(grads):
                begin = index * third + head * DH
                if shard == 0:
                    three_own[:, begin : begin + DH] = grad.astype(BF)
                else:
                    three_cross[:, begin : begin + DH] = grad.astype(BF)
    small_sums[:7, :] = sums_in[:7, :]
    small_sums[7:8, :] = slope_row
    arrive(qkv_o, qkv_t)
    own = three_own[...]
    other = three_cross[...]
    for index in range(width // TILE):
        at = columns(index)
        part[:, at] = (times_back(own, qkv_o[at, :]) + times_back(other, qkv_t[at, :])).astype(BF)


def k_ffn_one_back(
    info, mine, theirs, stream, small, grad_in, hidden, up_o, up_t, down_o, down_t,
    grad_out, gain_sum, branch, grad_cross, grad_own, part_own, part_sent, whole,
):
    high = info[1]
    rows, width = stream.shape
    span = rows // 2
    arrive(stream)

    def pass_back(at, first, carry):
        unit_rows, inverse = norm_unit(stream[at, :])
        grad, fresh = norm_back(pair_sum(mine, theirs, at), unit_rows, inverse, small[2:3, :])
        grad = grad_in[at, :] + grad
        grad_out[at, :] = grad
        branch[at, :] = (0.5 * grad).astype(BF)
        return carry + fresh

    gain_sum[...] = over_rows(rows, pass_back, jnp.zeros((1, width), F32))
    ffn_grad_hidden(branch, (down_o, down_t), hidden, grad_own, grad_cross)

    def store(at, values):
        whole[:, at] = values

    ffn_grad_input(grad_own, grad_cross, (up_o, up_t), store)
    part_own[...] = whole[pl.ds(high * span, span), :]
    part_sent[...] = whole[pl.ds((1 - high) * span, span), :].astype(BF)


def k_last(
    info, starts, part_own, arrived, frames, small, grad_in,
    grad_own, grad_sent, sums, grads,
):
    core, high, length = info[0], info[1], info[2]
    span, width = part_own.shape
    arrive(frames)

    def pass_back(at, first, carry):
        begin = pl.multiple_of(high * span + first, STEP)
        mask = mask_col(starts, begin, STEP, length)
        unit_rows, inverse = norm_unit(
            masked_rows(frames[pl.ds(begin, STEP), :], mask, small[0:1, :])
        )
        grad_normed = part_own[at, :] + arrived[at, :].astype(F32)
        grad, fresh = norm_back(grad_normed, unit_rows, inverse, small[1:2, :])
        grad = grad_in[pl.ds(begin, STEP), :] + grad
        hit = jnp.broadcast_to(mask, grad.shape) > 0.5
        grads[at, :] = jnp.where(hit, 0.0, grad)
        masked_part = jnp.sum(jnp.where(hit, grad, 0.0), axis=0, keepdims=True)
        return carry[0] + masked_part, carry[1] + fresh

    zero = jnp.zeros((1, width), F32)
    mask_sum, gain_sum = over_rows(span, pass_back, (zero, zero))
    sums[0:1, :] = mask_sum
    sums[1:2, :] = gain_sum
    rows = span // 2
    grad_own[...] = grads[pl.ds(core * rows, rows), :]
    grad_sent[...] = grads[pl.ds((1 - core) * rows, rows), :]


def k_weights(pairs, bit, tiles, info, *refs):
    count = 1 + max(max(pair[place] for place in (0, 1, 2, 4)) for pair in pairs)
    inputs, kept, sent = refs[:count], refs[count], refs[count + 1]
    mine = (info[3] >> bit) & 1
    low = bit - tiles
    rows = kept.shape[1]

    def one(index, carry):
        for side in range(2):
            tile = ((index >> low) * 2 + (mine ^ side)) * (1 << low) + (index & ((1 << low) - 1))
            at = pl.ds(pl.multiple_of(tile * rows, rows), rows)
            begin = 0
            for left, left_too, right, shift, right_too, shift_too, size in pairs:
                for piece in range(0, size, TILE):
                    grad = inner_rows(
                        inputs[left][:, at],
                        inputs[right][:, shift + piece : shift + piece + TILE],
                    ) + inner_rows(
                        inputs[left_too][:, at],
                        inputs[right_too][:, shift_too + piece : shift_too + piece + TILE],
                    )
                    spot = slice(begin + piece, begin + piece + TILE)
                    if side == 0:
                        kept[index, :, spot] = grad
                    else:
                        sent[index, :, spot] = grad.astype(BF)
                begin += size
        return carry

    lax.fori_loop(0, kept.shape[0], one, 0, unroll=2)


def k_fold(bit, count, info, held, *refs):
    arrivals, kept, sent = refs[:count], refs[count], refs[count + 1]
    mine = (info[3] >> bit) & 1
    for index in range(held.shape[0]):
        for side in range(2):
            at = pl.ds(mine ^ side, 1)
            begin = 0
            for entry in arrivals:
                spot = slice(begin, begin + entry.shape[3])
                total = held[index, at, :, spot][0] + entry[index, at][0].astype(F32)
                if side == 0:
                    kept[index, :, spot] = total
                else:
                    sent[index, :, spot] = total.astype(BF)
                begin = spot.stop


def k_finish(turned, count, info, kept, *refs):
    arrivals, results = refs[:count], refs[count:]
    cut = arrivals[0].shape[1]
    begin = 0
    for result, turn in zip(results, turned):
        size = result.shape[0] if turn else result.size // result.shape[0]
        for piece in range(begin, begin + size, DH):
            spot = slice(piece, piece + DH)
            at = piece - begin
            inside = slice(piece % cut, piece % cut + DH)
            total = kept[:, spot] + arrivals[piece // cut][:, inside].astype(F32)
            if turn:
                result[at : at + DH, :] = total.T
            elif len(result.shape) == 3:
                result[:, at // result.shape[2], pl.ds(at % result.shape[2], DH)] = total
            else:
                result[:, at : at + DH] = total
        begin += size


def k_in_order(info, own, other, result):
    core = info[0]
    result[pl.ds(core, 1)] = own[...][None]
    result[pl.ds(1 - core, 1)] = other[...][None]


def k_gather(bit, info, held, arrived, result):
    mine = (info[3] >> bit) & 1
    result[:, pl.ds(mine, 1)] = held[...][:, None]
    result[:, pl.ds(1 - mine, 1)] = arrived[...][:, None]


def k_smalls(last, attn, conv, two, final, channel_sums, result):
    width = attn.shape[1]
    result[0:2, :width] = last[...]
    for place, entry in enumerate((attn, conv, two, final), 2):
        result[place : place + 1, :width] = 0.5 * entry[...]
    result[6:8, :width] = jnp.zeros((2, width), F32)
    result[:, width:] = channel_sums[...]


def k_smalls_cross(smalls, result):
    width = smalls.shape[1] - 2 * (smalls.shape[1] - result.shape[1])
    channels = result.shape[1] - width
    result[:, :width] = smalls[:, :width]
    result[:, width:] = smalls[:, width + channels :]


def k_gains(mine, theirs, channel_sums, result):
    width = mine.shape[1]
    result[:, :width] = mine[...] + theirs[...]
    result[:, width:] = channel_sums[...]


def k_smalls_add(smalls, arrived, result):
    size = result.shape[1]
    result[...] = smalls[:, :size] + arrived[...]


def run(kernel, results, arguments, scalars=1, scratch=(), late=(), leaving=(), cost=1):
    given, made = len(arguments), len(results)
    hbm_shapes = [(arguments[place].shape, arguments[place].dtype) for place in late]
    hbm_shapes += [results[place] for place in leaving]
    buffers = [pltpu.VMEM(shape, kind) for shape, kind in hbm_shapes]
    own = [pltpu.VMEM(shape, kind) for shape, kind in scratch]
    hbm = pl.BlockSpec(memory_space=pltpu.HBM)

    def body(*refs):
        ins, outs = list(refs[:given]), list(refs[given : given + made])
        rest = refs[given + made :]
        extra, held, semaphores = rest[: len(own)], rest[len(own) : -1], rest[-1]
        for index, place in enumerate(late):
            ins[place] = Late(ins[place], held[index], semaphores.at[index])
        for index, place in enumerate(leaving, len(late)):
            outs[place] = Leaving(outs[place], held[index], semaphores.at[index])
        kernel(*ins, *outs, *extra)
        arrive(*ins)
        for place in leaving:
            outs[place].finish()

    def plain(*refs):
        kernel(*refs)

    held_bytes = sum(
        functools.reduce(lambda a, b: a * b, shape) * jnp.dtype(kind).itemsize
        for shape, kind in [*scratch, *hbm_shapes]
    )
    specs = [SMEM_SPEC] * scalars + [VMEM_SPEC] * (given - scalars)
    out_specs = [VMEM_SPEC] * made
    for place in late:
        specs[place] = hbm
    for place in leaving:
        out_specs[place] = hbm
    many = len(hbm_shapes)
    return pl.pallas_call(
        body if many else plain,
        out_shape=[
            pltpu.HBM(shape, kind) if place in leaving else pltpu.VMEM(shape, kind)
            for place, (shape, kind) in enumerate(results)
        ],
        in_specs=specs,
        out_specs=out_specs,
        scratch_shapes=own + buffers + ([pltpu.SemaphoreType.DMA((many,))] if many else []),
        compiler_params=pltpu.CompilerParams(vmem_limit_bytes=held_bytes + 8 * MIB),
        cost_estimate=pl.CostEstimate(flops=cost, bytes_accessed=cost, transcendentals=0),
    )(*(
        entry if place < scalars else pltpu.with_memory_space_constraint(
            entry, pltpu.HBM if place in late else pltpu.VMEM
        )
        for place, entry in enumerate(arguments)
    ))


def swap(value, axis, bit):
    size = lax.axis_size(axis)
    return lax.ppermute(value, axis, [(place, place ^ bit) for place in range(size)])


def across(value):
    return swap(value, "tensor", 2)


def beside(value):
    return swap(value, "tensor", 1)


def bit_of(axis, bit):
    return (lax.axis_index(axis) & bit) != 0


def tie(*values):
    return lax.optimization_barrier(values)


class RowSum:
    def __init__(self, info, inputs, pairs, width, first_bits, cuts=(), cost=1):
        size = lax.axis_size("dp")
        levels = size.bit_length() - 1
        tiles = max(levels - 3, 0)
        order = [tiles + bit for bit in first_bits]
        self.order = order + [bit for bit in range(levels - 1, -1, -1) if bit not in order]
        self.left = list(range(levels - 1, -1, -1))
        self.total = sum(pair[-1] for pair in pairs)
        self.block = width // size
        self.info = info
        count = size >> tiles
        shape = (count // 2, width // count)
        self.kept, *self.sent = run(
            functools.partial(k_weights, pairs, self.order[0], tiles),
            [((*shape, self.total), F32)]
            + [((*shape, size), BF) for size in (cuts or (self.total,))],
            [info] + inputs,
            cost=cost,
        )
        self.begin()

    def begin(self):
        self.bit = self.order.pop(0)
        self.left.remove(self.bit)
        self.arrived = []

    def send(self, chain=None):
        piece = self.sent.pop(0)
        if chain is not None:
            (piece,) = chain.after(piece)
        self.arrived.append(swap(piece, "dp", 1 << self.bit))

    def here(self, chain):
        (self.arrived[-1],) = chain.after(self.arrived[-1])

    def fold(self, chain, cost=1):
        bit = self.order[0]
        place = self.left.index(bit)
        inner = self.block << (len(self.left) - 1 - place)
        outer = 1 << place
        kept, *arrived = chain.after(self.kept, *self.arrived)
        self.kept, *self.sent = run(
            functools.partial(k_fold, bit, len(arrived)),
            [((outer, inner, self.total), F32), ((outer, inner, self.total), BF)],
            [self.info, kept.reshape(outer, 2, inner, self.total)]
            + [entry.reshape(outer, 2, inner, -1) for entry in arrived],
            cost=cost,
        )
        self.kept, chain.last = tie(self.kept, chain.last)
        self.begin()

    def step(self, chain, cost=1):
        self.fold(chain, cost=cost)
        self.send()

    def finish(self, chain, *results):
        while self.order:
            self.step(chain)
        shape = (self.block, self.total)
        kept, *arrived = chain.after(
            self.kept.reshape(shape), *(entry.reshape(self.block, -1) for entry in self.arrived)
        )
        sums = run(
            functools.partial(k_finish, tuple(turn for _, turn in results), len(arrived)),
            [(size, F32) for size, _ in results],
            [self.info, kept, *arrived],
        )
        *sums, chain.last = tie(*sums, chain.last)
        return sums


class Chain:
    def __init__(self, last):
        self.last = last

    def after(self, *values):
        *values, self.last = tie(*values, self.last)
        return values


class Gather:
    def __init__(self, info, block):
        self.info, self.held = info, block.reshape(1, *block.shape)
        self.bit = lax.axis_size("dp") // 2
        self.shape = (lax.axis_size("dp") * block.shape[0], block.shape[1])

    def send(self):
        self.arrived = swap(self.held, "dp", self.bit)

    def take(self):
        outer, rows, width = self.held.shape
        (held,) = run(
            functools.partial(k_gather, self.bit.bit_length() - 1),
            [((outer, 2, rows, width), self.held.dtype)],
            [self.info, self.held, self.arrived],
        )
        self.held = held.reshape(outer * 2, rows, width)
        self.bit //= 2

    def whole(self):
        while self.bit:
            self.send()
            self.take()
        return self.held.reshape(self.shape)


def sum_pair(value, axis, merge=None):
    bit, size = 1, lax.axis_size(axis)
    while bit * 2 < size:
        (value,) = run(
            merge or k_add, [(value.shape, F32)], [value, swap(value, axis, bit)], scalars=0
        )
        bit *= 2
    return value, swap(value, axis, bit)


def per_device(
    frames,
    lengths,
    span_starts,
    mask_vector,
    ffn1_gain,
    ffn1_up,
    ffn1_down,
    attn_gain,
    query_weight,
    key_weight,
    value_weight,
    output_weight,
    rel_slope,
    conv_gain,
    conv_up,
    conv_depth,
    bn_scale,
    bn_shift,
    conv_down,
    ffn2_gain,
    ffn2_up,
    ffn2_down,
    final_gain,
    cotangent,
):
    batches, row_count, width = frames.shape
    length = row_count * lax.axis_size("tensor")
    span = 2 * row_count
    channels = conv_depth.shape[1]
    hidden_width = ffn1_up.shape[1]
    heads = rel_slope.shape[0]
    third = query_weight.shape[1]
    core = lax.axis_index("tensor") & 1
    high = (lax.axis_index("tensor") >> 1) & 1
    group = lax.axis_index("dp")
    on_first = core == 0
    own_length = jnp.where(on_first, lengths[0], lengths[1])
    info = jnp.stack([core, high, own_length, group]).astype(jnp.int32)
    starts = jnp.where(on_first, span_starts[0:1], span_starts[1:2])

    frames_across = across(frames)
    conv_block = jnp.concatenate(
        [conv_up.reshape(conv_up.shape[0], 2 * channels), conv_down.T], axis=1
    )
    conv_weights = Gather(info, conv_block)
    conv_weights.send()

    part = mask_vector.shape[0]
    place = (group * lax.axis_size("tensor") + lax.axis_index("tensor")) * part
    vectors = jnp.stack(
        [mask_vector.astype(F32), ffn1_gain, attn_gain, conv_gain, ffn2_gain, final_gain,
         jnp.zeros_like(ffn1_gain), jnp.zeros_like(ffn1_gain)]
    )
    small = lax.dynamic_update_slice(jnp.zeros((8, width), F32), vectors, (0, place))
    hops = [("tensor", 1), ("dp", 2), ("dp", 1), ("tensor", 2)]
    bit = 4
    while bit < lax.axis_size("dp"):
        hops.append(("dp", bit))
        bit *= 2
    for step, (axis, bit) in enumerate(hops):
        if step == 4:
            (sent,) = run(k_pick, [(frames.shape, BF)], [info, frames, frames_across])
            sent, small = tie(sent, small)
        if step == 3:
            query_weight, key_weight, conv_depth, rel_slope, small = tie(
                query_weight, key_weight, conv_depth, rel_slope, small
            )
            own_qkv = jnp.concatenate([query_weight, key_weight, value_weight], axis=1)
            slope_row = jnp.pad(rel_slope[None], ((0, 0), (0, channels - heads)))
            own_params = jnp.concatenate([conv_depth, bn_scale[None], bn_shift[None], slope_row])
            other_params = beside(own_params)
            conv_weights.arrived, small = tie(conv_weights.arrived, small)
            conv_weights.take()
            if conv_weights.bit:
                conv_weights.send()
        if bit < lax.axis_size(axis):
            (small,) = run(
                k_add, [(small.shape, F32)], [small, swap(small, axis, bit)], scalars=0
            )
    if conv_weights.bit:
        conv_weights.arrived, small = tie(conv_weights.arrived, small)
        conv_weights.take()
    frame_parts = [frames, frames_across, beside(sent)]
    own_qkv, other_params, conv_weights.held, small = tie(
        own_qkv, other_params, conv_weights.held, small
    )
    params = jnp.concatenate([own_params, other_params], axis=1)
    slopes = jnp.concatenate([rel_slope, other_params[KW + 2, :heads]])
    if conv_weights.bit:
        conv_weights.send()
    up_one, down_one = beside(ffn1_up), beside(ffn1_down)

    wide = (length, width)
    ffn_outs = [
        (wide, BF),
        ((length, hidden_width), BF),
        ((length, hidden_width), BF),
        ((length, 2 * hidden_width), F32),
        (wide, BF),
    ]
    whole, norm_one, cross_one, active_one, hidden_one, partial = run(
        k_ffn_one,
        [(wide, BF)] + ffn_outs,
        [info, starts, *frame_parts, small, ffn1_up, up_one, ffn1_down, down_one],
        scratch=[(wide, BF)], late=(6, 8),
    )
    output_weight, active_one = tie(output_weight, active_one)
    other_qkv, other_out = beside(own_qkv), beside(output_weight)
    stream_one, norm_attn, context_cross, context_own, qkv, weights, partial = run(
        k_attn_wrapped,
        [
            (wide, F32),
            (wide, BF),
            ((length, third), BF),
            ((length, third), BF),
            ((length, 6 * third), BF),
            ((2 * heads, length, length), F32),
            (wide, BF),
        ],
        [info, slopes, starts, partial, across(partial), whole, small, own_qkv, other_qkv,
         output_weight, other_out],
        scalars=2, late=(7, 9),
    )
    conv_weights.arrived, norm_one, cross_one, context_own = tie(
        conv_weights.arrived, norm_one, cross_one, context_own
    )
    conv_weights.take()
    own_conv = conv_weights.whole()
    other_conv = beside(own_conv)
    norm_one_too, cross_one_too = beside(norm_one), beside(cross_one)
    norm_one_too, cross_one_too, params = tie(norm_one_too, cross_one_too, params)
    both_channels = (length, 2 * channels)
    stat_shape = ((8, 2 * channels), F32)
    stream_two, norm_conv, value, gate, padded, convolved, stats = run(
        k_conv_front,
        [
            (wide, F32),
            (wide, BF),
            (both_channels, F32),
            (both_channels, F32),
            ((length + 2 * EDGE, 2 * channels), F32),
            (both_channels, F32),
            stat_shape,
        ],
        [info, partial, across(partial), stream_one, small, params, own_conv, other_conv],
        late=(6,),
    )
    norm_attn, context_cross, cotangent, ffn2_up, ffn2_down, value = tie(
        norm_attn, context_cross, cotangent, ffn2_up, ffn2_down, value
    )
    stats, stats_too = sum_pair(stats, "dp", k_merge)
    grad_across = across(cotangent)
    up_two, down_two = beside(ffn2_up), beside(ffn2_down)
    norm_attn_too, context_cross_too = beside(norm_attn), beside(context_cross)
    params, grad_across = tie(params, grad_across)
    stats, active_conv, cross_conv, partial = run(
        k_conv_rear,
        [stat_shape, ((length, channels), BF), ((length, channels), BF), (wide, BF)],
        [stats, stats_too, convolved, params, norm_conv, own_conv, other_conv],
        scalars=0, late=(5,),
    )
    grad_across, active_conv = tie(grad_across, active_conv)
    (sent,) = run(k_pick, [(cotangent.shape, BF)], [info, cotangent, grad_across])
    grad_parts = [cotangent, grad_across, beside(sent)]
    grad_parts[2], small = tie(grad_parts[2], small)
    stream_three, norm_two, cross_two, active_two, hidden_two, partial = run(
        k_ffn_two,
        [(wide, F32)] + ffn_outs,
        [partial, across(partial), stream_two, small, ffn2_up, up_two, ffn2_down, down_two],
        scalars=0, late=(4, 6),
    )
    norm_two, cross_two, norm_conv, cross_conv, active_two = tie(
        norm_two, cross_two, norm_conv, cross_conv, active_two
    )
    norm_two_too, cross_two_too = beside(norm_two), beside(cross_two)
    norm_conv_too, cross_conv_too = beside(norm_conv), beside(cross_conv)
    (
        norm_two_too, cross_two_too, norm_conv_too, cross_conv_too, norm_attn_too,
        context_cross_too, small,
    ) = tie(
        norm_two_too, cross_two_too, norm_conv_too, cross_conv_too, norm_attn_too,
        context_cross_too, small,
    )

    row_shape = ((1, width), F32)
    block_shape = (row_count, width)
    out_own, out_sent, grad_four, sum_final, back_two, hid_cross_two, hid_two, partial = run(
        k_ffn_two_back,
        [
            (block_shape, BF),
            (block_shape, BF),
            (wide, F32),
            row_shape,
            (wide, BF),
            ((length, hidden_width), BF),
            ((length, hidden_width), BF),
            (wide, BF),
        ],
        [info, partial, across(partial), stream_three, small, *grad_parts, hidden_two,
         ffn2_up, up_two, ffn2_down, down_two],
        scratch=[(wide, BF), (wide, BF)], late=(9, 11),
    )
    back_two_too, hid_cross_two_too = beside(back_two), beside(hid_cross_two)
    ffn_pair = ((0, 1, 2, 0, 3, 0, hidden_width),)
    two_up = RowSum(
        info, [norm_two, norm_two_too, hid_two, hid_cross_two_too], ffn_pair, width, (0, 1, 2)
    )
    two_down = RowSum(
        info, [back_two, back_two_too, active_two, cross_two_too], ffn_pair, width, (1, 2, 0)
    )
    grad_four, two_up.sent[0], two_down.sent[0] = tie(
        grad_four, two_up.sent[0], two_down.sent[0]
    )
    grad_three, sum_two, back_conv, grad_shaped, sums = run(
        k_conv_back_front,
        [(wide, F32), row_shape, (wide, BF), (both_channels, F32), stat_shape],
        [partial, across(partial), stream_three, small, grad_four, convolved, stats, params,
         own_conv, other_conv],
        scalars=0, late=(8,),
    )
    out_sent, sum_two, back_conv = tie(out_sent, sum_two, back_conv)
    out_other, back_conv_too = beside(out_sent), beside(back_conv)
    bits = [1 << level for level in range(lax.axis_size("dp").bit_length() - 1)]
    for bit in bits[:-1]:
        (sums,) = run(
            k_add, [(sums.shape, F32)], [sums, swap(sums, "dp", bit)], scalars=0
        )
        chain = Chain(sums)
        if bit == 1:
            two_up.send(chain)
        if bit == 2:
            two_down.send(chain)
        sums = chain.last
    sums_too = swap(sums, "dp", bits[-1])
    sums_too, out_other, back_conv_too = tie(sums_too, out_other, back_conv_too)
    small_sums, mixed_own, mixed_cross, partial = run(
        k_conv_back_rear,
        [
            stat_shape,
            ((length, 2 * channels), BF),
            ((length, 2 * channels), BF),
            (wide, BF),
        ],
        [info, sums, sums_too, grad_shaped, convolved, stats, params, padded, value, gate,
         back_conv, own_conv, other_conv],
        scratch=[((length + 2 * EDGE, 2 * channels), F32)], late=(11,),
    )
    mixed_cross_too = beside(mixed_cross)
    mixed_cross_too, grad_three = tie(mixed_cross_too, grad_three)
    grad_two, sum_conv, back_attn, three_cross, three_own, small_sums, partial = run(
        k_attn_back,
        [
            (wide, F32),
            row_shape,
            (wide, BF),
            ((length, 3 * third), BF),
            ((length, 3 * third), BF),
            stat_shape,
            (wide, BF),
        ],
        [partial, across(partial), stream_two, small, grad_three, small_sums, qkv, weights,
         own_qkv, other_qkv, output_weight, other_out],
        scalars=0,
        scratch=[((length, 2 * third), BF)], late=(8, 10),
    )
    back_attn_too, three_cross_too = beside(back_attn), beside(three_cross)
    chain = Chain(small_sums)
    for entry in (two_up, two_down):
        entry.step(chain)
    back_attn, three_own = chain.after(back_attn, three_own)
    small_sums = chain.last
    middle = RowSum(
        info,
        [norm_conv, norm_conv_too, mixed_own, mixed_cross_too,
         back_conv, back_conv_too, active_conv, cross_conv_too,
         norm_attn, norm_attn_too, three_own, three_cross_too,
         back_attn, back_attn_too, context_own, context_cross_too],
        (
            (0, 1, 2, 0, 3, 0, 2 * channels),
            (4, 5, 6, 0, 7, 0, channels),
            (8, 9, 10, 0, 11, 0, 3 * third),
            (12, 13, 14, 0, 15, 0, third),
        ),
        width, (0, 1, 2),
    )
    middle.send()
    middle.kept, grad_two = tie(middle.kept, grad_two)
    grad_one, sum_attn, back_one, hid_cross_one, hid_one, last_own, last_sent = run(
        k_ffn_one_back,
        [
            (wide, F32),
            row_shape,
            (wide, BF),
            ((length, hidden_width), BF),
            ((length, hidden_width), BF),
            ((span, width), F32),
            ((span, width), BF),
        ],
        [info, partial, across(partial), stream_one, small, grad_two, hidden_one,
         ffn1_up, up_one, ffn1_down, down_one],
        scratch=[(wide, F32)], late=(7, 9),
    )
    back_one_too, hid_cross_one_too = beside(back_one), beside(hid_cross_one)
    chain = Chain(sum_attn)
    for entry in (two_up, two_down):
        entry.step(chain, cost=COST)
    hid_one, active_one = chain.after(hid_one, active_one)
    one_up = RowSum(
        info, [norm_one, norm_one_too, hid_one, hid_cross_one_too], ffn_pair, width, (0, 1, 2),
        cost=COST,
    )
    one_down = RowSum(
        info, [back_one, back_one_too, active_one, cross_one_too], ffn_pair, width, (0, 1, 2),
        cost=COST,
    )
    one_up.send(chain)
    one_up.kept, chain.last = tie(one_up.kept, chain.last)
    one_down.send(chain)
    one_down.kept, chain.last = tie(one_down.kept, chain.last)
    block = width // lax.axis_size("dp")
    (starts,) = chain.after(starts)
    sum_attn = chain.last
    frames_own, frames_sent, last_sums = run(
        k_last,
        [(block_shape, F32), (block_shape, F32), ((2, width), F32)],
        [info, starts, last_own, across(last_sent), whole, small, grad_one],
        scratch=[((span, width), F32)],
    )
    frames_other = beside(frames_sent)
    (smalls,) = run(
        k_smalls, [((8, width + 2 * channels), F32)],
        [last_sums, sum_attn, sum_conv, sum_two, sum_final, small_sums], scalars=0,
    )
    (smalls_sent,) = run(k_smalls_cross, [((8, width + channels), F32)], [smalls], scalars=0)
    (smalls,) = run(
        k_smalls_add, [((8, width + channels), F32)], [smalls, beside(smalls_sent)], scalars=0
    )
    gains, gains_too = smalls[:, :width], across(smalls[:, :width])
    (gains,) = run(
        k_gains, [(smalls.shape, F32)], [gains, gains_too, smalls[:, width:]], scalars=0
    )

    def in_order(own, other):
        return run(k_in_order, [((2, *own.shape), own.dtype)], [info, own, other])[0]

    chain = Chain(in_order(out_own, out_other))

    def hop(value, bit):
        (value,) = chain.after(value)
        return value, swap(value, "dp", bit)

    def add(value, other):
        (total,) = run(k_add, [(value.shape, F32)], chain.after(value, other), scalars=0)
        return total

    first, *between = [1 << level for level in range(1, lax.axis_size("dp").bit_length() - 1)]
    gains = add(*hop(gains, first))
    gains, chain.last = tie(gains, chain.last)
    (two_up,) = two_up.finish(chain, ((block, hidden_width), False))
    middle.step(chain)
    for bit in between:
        gains = add(*hop(gains, bit))
    gains, chain.last = tie(gains, chain.last)
    middle.step(chain)
    one_up.step(chain)
    one_down.step(chain)
    one_up.step(chain)
    conv_up_grad, conv_down_grad, query_grad, key_grad, value_grad, output_grad = middle.finish(
        chain,
        (conv_up.shape, False), ((channels, block), True),
        *[((block, third), False)] * 3, ((third, block), True),
    )
    gains, gains_too = hop(gains, 1)
    (one_up,) = one_up.finish(chain, ((block, hidden_width), False))
    gains = add(gains, gains_too)
    one_down.step(chain)
    (two_down,) = two_down.finish(chain, ((hidden_width, block), True))
    channel_sums = gains[:, width:]
    scale_grad = channel_sums[KW + 1] * (1.0 / lax.axis_size("dp"))
    shift_grad = channel_sums[KW] * (1.0 / lax.axis_size("dp"))
    gains = lax.dynamic_slice_in_dim(gains, place, part, axis=1)

    frames_grad = in_order(frames_own, frames_other)
    smallest = [
        *(gains[index] for index in range(6)),
        channel_sums[KW + 2, :heads],
        channel_sums[:KW],
        scale_grad,
        shift_grad,
    ]
    frames_grad, *smallest = chain.after(frames_grad, *smallest)
    (one_down,) = one_down.finish(chain, ((hidden_width, block), True))

    return (
        chain.last,
        frames_grad,
        smallest[0],
        smallest[1],
        one_up,
        one_down,
        smallest[2],
        query_grad,
        key_grad,
        value_grad,
        output_grad,
        smallest[6],
        smallest[3],
        conv_up_grad,
        smallest[7],
        smallest[8],
        smallest[9],
        conv_down_grad,
        smallest[4],
        two_up,
        two_down,
        smallest[5],
    )


def k_attn_wrapped(info, slopes, starts, *refs):
    k_attn(info, starts, slopes, *refs)


def solution(mesh):
    every, split, by_column = P(("dp", "tensor")), P("tensor"), P(None, "tensor")
    rows_by = P("dp", "tensor", None)
    return jax.shard_map(
        per_device,
        mesh=mesh,
        in_specs=(
            rows_by,
            P("dp"),
            P("dp", None),
            every,
            every,
            by_column,
            P("tensor", None),
            every,
            by_column,
            by_column,
            by_column,
            P("tensor", None),
            split,
            every,
            P("dp", None, "tensor"),
            by_column,
            split,
            split,
            P("tensor", "dp"),
            every,
            by_column,
            P("tensor", None),
            every,
            rows_by,
        ),
        out_specs=(
            rows_by,
            rows_by,
            every,
            every,
            P("dp", "tensor"),
            P("tensor", "dp"),
            every,
            P("dp", "tensor"),
            P("dp", "tensor"),
            P("dp", "tensor"),
            P("tensor", "dp"),
            split,
            every,
            P("dp", None, "tensor"),
            by_column,
            split,
            split,
            P("tensor", "dp"),
            every,
            P("dp", "tensor"),
            P("tensor", "dp"),
            every,
        ),
        check_vma=False,
    )
```

profile of v0, /device:TPU:0, one launch (start us, length us, event | category | flops | bytes accessed | tf_op | source)
XLA Modules:
  0.0 320.3 jit_solution(11344879771825089949)
XLA Ops:
  5.4 3.7 %collective-permute-start.4 = (bf16[1,128,768]{2,1,0:T(8,128)(2,1)S(1)}, bf16[1,128,768]{2,1,0:T(8,128)(2,1)S(1)}, u32[]{:S(2)}, u32[]{:S(2)}) collective-permute-start(bf16[1,128,768]{2,1,0:T(8,128)(2,1)S(1)} %maximum_bitcast_fusion.refs_1_), channel_id=1, source_target_pairs={{0,16},{4,20},{8,24},{12,28},{16,0},{20,4},{24,8},{28,12},{1,17},{... | collective-permute-start | bytes 589832 | tf_op jit(solution)/shard_map/ppermute | solution.py:843
  16.5 2.4 collective-permute-done.2.refs_1_
  19.5 2.2 collective-permute-start.5
  26.8 2.0 collective-permute-start.8
  28.9 2.8 collective-permute-done.8.refs_1_
  36.2 5.9 %shard_map.407 = (bf16[256,1024]{1,0:T(8,128)(2,1)S(1)}, bf16[256,1024]{1,0:T(8,128)(2,1)S(1)}, bf16[256,1024]{1,0:T(8,128)(2,1)S(1)}, bf16[256,1024]{1,0:T(8,12...) custom-call(s32[4]{0:T(128)S(1)} %pad_add_fusion.refs_0_, ...), custom_call_target="tpu_custom_call" | custom-call | flops 1 | bytes 1 | tf_op jit(solution)/shard_map/pallas_call | solution.py:822
  44.1 12.4 %collective-permute-done.12.refs_4_ = bf16[256,1024]{1,0:T(8,128)(2,1)S(1)} collective-permute-done((bf16[256,1024]{1,0:T(8,128)(2,1)S(1)}, bf16[256,1024]{1,0:T(8,128)(2,1)S(1)}, u32[]{:S(2)}, u32[]{:S(2)}) %collective-permute-start.12) | collective-permute-done | bytes 524320 | tf_op jit(solution)/shard_map/ppermute | solution.py:843
  56.5 4.2 %shard_map.408 = (f32[256,1024]{1,0:T(8,128)S(1)}, bf16[256,1024]{1,0:T(8,128)(2,1)S(1)}, bf16[256,256]{1,0:T(8,128)(2,1)S(1)}, bf16[256,256]{1,0:T(8,128)(2,1)S...) custom-call(s32[4]{0:T(128)S(1)} %pad_add_fusion.refs_0_, ...), custom_call_target="tpu_custom_call" | custom-call | flops 1 | bytes 1 | tf_op jit(solution)/shard_map/pallas_call | solution.py:822
  63.6 2.0 collective-permute-done.18.refs_4_
  66.4 10.0 %collective-permute-done.15.refs_2_ = bf16[256,1024]{1,0:T(8,128)(2,1)S(1)} collective-permute-done((bf16[256,1024]{1,0:T(8,128)(2,1)S(1)}, bf16[256,1024]{1,0:T(8,128)(2,1)S(1)}, u32[]{:S(2)}, u32[]{:S(2)}) %collective-permute-start.15) | collective-permute-done | bytes 524320 | tf_op jit(solution)/shard_map/ppermute | solution.py:843
  76.4 3.5 %shard_map.410 = (f32[256,1024]{1,0:T(8,128)S(1)}, bf16[256,1024]{1,0:T(8,128)(2,1)S(1)}, f32[256,512]{1,0:T(8,128)S(1)}, f32[256,512]{1,0:T(8,128)S(1)}, f32[27...) custom-call(s32[4]{0:T(128)S(1)} %pad_add_fusion.refs_0_, ...), custom_call_target="tpu_custom_call" | custom-call | flops 1 | bytes 1 | tf_op jit(solution)/shard_map/pallas_call | solution.py:822
  83.5 2.2 collective-permute-done.20.refs_1_
  85.8 1.9 collective-permute-start.21
  89.6 2.0 collective-permute-start.22
  91.5 2.7 collective-permute-done.22.refs_1_
  99.1 8.1 %collective-permute-done.24.refs_1_ = bf16[256,1024]{1,0:T(8,128)(2,1)S(1)} collective-permute-done((bf16[256,1024]{1,0:T(8,128)(2,1)S(1)}, bf16[256,1024]{1,0:T(8,128)(2,1)S(1)}, u32[]{:S(2)}, u32[]{:S(2)}) %collective-permute-start.24) | collective-permute-done | bytes 524320 | tf_op jit(solution)/shard_map/ppermute | solution.py:843
  107.1 4.3 %shard_map.415 = (f32[256,1024]{1,0:T(8,128)S(1)}, bf16[256,1024]{1,0:T(8,128)(2,1)S(1)}, bf16[256,1024]{1,0:T(8,128)(2,1)S(1)}, bf16[256,1024]{1,0:T(8,128)(2,1...) custom-call(bf16[256,1024]{1,0:T(8,128)(2,1)S(1)} %get-tuple-element.350.refs_0_, ...), custom_call_target="tpu_custom_call" | custom-call | flops 1 | bytes 1 | tf_op jit(solution)/shard_map/pallas_call | solution.py:822
  112.6 2.5 collective-permute-done.32.refs_8_
  115.1 11.3 %collective-permute-done.28.refs_2_ = bf16[256,1024]{1,0:T(8,128)(2,1)S(1)} collective-permute-done((bf16[256,1024]{1,0:T(8,128)(2,1)S(1)}, bf16[256,1024]{1,0:T(8,128)(2,1)S(1)}, u32[]{:S(2)}, u32[]{:S(2)}) %collective-permute-start.28) | collective-permute-done | bytes 524320 | tf_op jit(solution)/shard_map/ppermute | solution.py:843
  126.4 5.6 %shard_map.416 = (bf16[64,1024]{1,0:T(8,128)(2,1)S(1)}, bf16[64,1024]{1,0:T(8,128)(2,1)S(1)}, f32[256,1024]{1,0:T(8,128)S(1)}, f32[1,1024]{1,0:T(1,128)S(1)}, bf...) custom-call(s32[4]{0:T(128)S(1)} %pad_add_fusion.refs_0_, ...), custom_call_target="tpu_custom_call" | custom-call | flops 1 | bytes 1 | tf_op jit(solution)/shard_map/pallas_call | solution.py:822
  134.0 2.2 shard_map.418
  136.1 2.2 shard_map.417
  138.3 8.2 %collective-permute-done.37.refs_1_ = bf16[256,1024]{1,0:T(8,128)(2,1)S(1)} collective-permute-done((bf16[256,1024]{1,0:T(8,128)(2,1)S(1)}, bf16[256,1024]{1,0:T(8,128)(2,1)S(1)}, u32[]{:S(2)}, u32[]{:S(2)}) %collective-permute-start.37) | collective-permute-done | bytes 524320 | tf_op jit(solution)/shard_map/ppermute | solution.py:843
  146.5 2.2 shard_map.419
  150.8 2.2 collective-permute-done.38.refs_1_
  154.8 2.0 collective-permute-done.39.refs_1_
  161.7 2.7 shard_map.422
  166.4 8.9 %collective-permute-done.43.refs_1_ = bf16[256,1024]{1,0:T(8,128)(2,1)S(1)} collective-permute-done((bf16[256,1024]{1,0:T(8,128)(2,1)S(1)}, bf16[256,1024]{1,0:T(8,128)(2,1)S(1)}, u32[]{:S(2)}, u32[]{:S(2)}) %collective-permute-start.43) | collective-permute-done | bytes 524320 | tf_op jit(solution)/shard_map/ppermute | solution.py:843
  175.3 4.3 %shard_map.423 = (f32[256,1024]{1,0:T(8,128)S(1)}, f32[1,1024]{1,0:T(1,128)S(1)}, bf16[256,1024]{1,0:T(8,128)(2,1)S(1)}, bf16[256,768]{1,0:T(8,128)(2,1)S(1)}, b...) custom-call(bf16[256,1024]{1,0:T(8,128)(2,1)S(1)} %get-tuple-element.400.refs_0_, ...), custom_call_target="tpu_custom_call" | custom-call | flops 1 | bytes 1 | tf_op jit(solution)/shard_map/pallas_call | solution.py:822
  183.3 3.3 %shard_map.426 = (f32[4,128,1792]{2,1,0:T(8,128)S(1)}, bf16[4,128,1792]{2,1,0:T(8,128)(2,1)S(1)}) custom-call(s32[4]{0:T(128)S(1)} %pad_add_fusion.refs_0_, bf16[256,1024]{1,0:T(8,128)(2,1)S(1)} %get-tuple-element.366.refs_4_.refs_1_, bf16[256,1024]{1,0:T(8,128)(2,1)S(1)} %collective-permute-done.31.refs_2_, ...), custom_call_target="tpu_custom_call" | custom-call | flops 1 | bytes 1 | tf_op jit(solution)/shard_map/pallas_call | solution.py:822
  190.7 9.4 %collective-permute-done.45.refs_2_ = bf16[256,1024]{1,0:T(8,128)(2,1)S(1)} collective-permute-done((bf16[256,1024]{1,0:T(8,128)(2,1)S(1)}, bf16[256,1024]{1,0:T(8,128)(2,1)S(1)}, u32[]{:S(2)}, u32[]{:S(2)}) %collective-permute-start.45) | collective-permute-done | bytes 524320 | tf_op jit(solution)/shard_map/ppermute | solution.py:843
  200.1 6.8 %shard_map.427 = (f32[256,1024]{1,0:T(8,128)S(1)}, f32[1,1024]{1,0:T(1,128)S(1)}, bf16[256,1024]{1,0:T(8,128)(2,1)S(1)}, bf16[256,1024]{1,0:T(8,128)(2,1)S(1)}, ...) custom-call(s32[4]{0:T(128)S(1)} %pad_add_fusion.refs_0_, ...), custom_call_target="tpu_custom_call" | custom-call | flops 1 | bytes 1 | tf_op jit(solution)/shard_map/pallas_call | solution.py:822
  207.4 2.8 collective-permute-done.52
  215.2 2.2 shard_map.431
  217.8 2.4 shard_map.430
  224.2 7.3 %collective-permute-start.60 = (f32[8,1024]{1,0:T(8,128)S(1)}, f32[8,1024]{1,0:T(8,128)S(1)}, u32[]{:S(2)}, u32[]{:S(2)}) collective-permute-start(f32[8,1024]{1,0:T(8,128)S(1)} %slice.74.refs_0_), channel_id=1, source_target_pairs={{0,2},{1,3},{2,0},{3,1},{4,6},{5,7},{6,4},{7,5},{8,10},{9,11},{10,... | collective-permute-start | bytes 98312 | tf_op jit(solution)/shard_map/ppermute | solution.py:843
  233.4 4.0 %collective-permute-done.61.refs_1_ = f32[8,1280]{1,0:T(8,128)S(1)} collective-permute-done((f32[8,1280]{1,0:T(8,128)S(1)}, f32[8,1280]{1,0:T(8,128)S(1)}, u32[]{:S(2)}, u32[]{:S(2)}) %collective-permute-start.61) | collective-permute-done | bytes 40992 | tf_op jit(solution)/shard_map/ppermute | solution.py:843
  239.0 2.1 collective-permute-start.54
  241.1 2.9 collective-permute-start.63
  244.0 14.7 %collective-permute-done.63.refs_1_ = f32[8,1280]{1,0:T(8,128)S(1)} collective-permute-done((f32[8,1280]{1,0:T(8,128)S(1)}, f32[8,1280]{1,0:T(8,128)S(1)}, u32[]{:S(2)}, u32[]{:S(2)}) %collective-permute-start.63) | collective-permute-done | bytes 40992 | tf_op jit(solution)/shard_map/ppermute | solution.py:843
  258.7 2.2 collective-permute-done.62
  262.4 3.0 collective-permute-start.66
  265.7 6.9 %collective-permute-done.54 = bf16[4,128,1024]{2,1,0:T(8,128)(2,1)S(1)} collective-permute-done((bf16[4,128,1024]{2,1,0:T(8,128)(2,1)S(1)}, bf16[4,128,1024]{2,1,0:T(8,128)(2,1)S(1)}, u32[]{:S(2)}, u32[]{:S(2)}) %collective-permute-start.54) | collective-permute-done | bytes 1048608 | tf_op jit(solution)/shard_map/ppermute | solution.py:843
  274.0 10.5 %collective-permute-done.66 = bf16[2,128,1024]{2,1,0:T(8,128)(2,1)S(1)} collective-permute-done((bf16[2,128,1024]{2,1,0:T(8,128)(2,1)S(1)}, bf16[2,128,1024]{2,1,0:T(8,128)(2,1)S(1)}, u32[]{:S(2)}, u32[]{:S(2)}) %collective-permute-start.66) | collective-permute-done | bytes 524320 | tf_op jit(solution)/shard_map/ppermute | solution.py:843
  286.2 2.5 collective-permute-start.64
  289.5 2.1 collective-permute-start.67
  300.2 4.0 %collective-permute-done.64 = bf16[2,128,1024]{2,1,0:T(8,128)(2,1)} collective-permute-done((bf16[2,128,1024]{2,1,0:T(8,128)(2,1)}, bf16[2,128,1024]{2,1,0:T(8,128)(2,1)}, u32[]{:S(2)}, u32[]{:S(2)}) %collective-permute-start.64) | collective-permute-done | bytes 524320 | tf_op jit(solution)/shard_map/ppermute | solution.py:843
  311.6 6.4 %collective-permute-done.69 = bf16[1,128,1024]{2,1,0:T(8,128)(2,1)S(1)} collective-permute-done((bf16[1,128,1024]{2,1,0:T(8,128)(2,1)S(1)}, bf16[1,128,1024]{2,1,0:T(8,128)(2,1)S(1)}, u32[]{:S(2)}, u32[]{:S(2)}) %collective-permute-start.69) | collective-permute-done | bytes 262176 | tf_op jit(solution)/shard_map/ppermute | solution.py:843
  (226 shorter events, 95.7 us)
Async XLA Ops:
  0.7 35.5 %collective-permute-start.10 = (bf16[1024,1024]{1,0:T(8,128)(2,1)}, bf16[1024,1024]{1,0:T(8,128)(2,1)S(1)}, u32[]{:S(2)}, u32[]{:S(2)}) collective-permute-start(bf16[1024,1024]{1,0:T(8,128)(2,1)} %refs_7_.1), channel_id=1, source_target_pairs={{0,1},{1,0},{2,3},{3,2},{4,5},{5,4},{6,7},{7,6},{8,9},{9,8},{10,11... | collective-permute-start | bytes 6291464 | tf_op jit(solution)/shard_map/ppermute | solution.py:843
  1.2 35.0 %collective-permute-start.11 = (bf16[1024,1024]{1,0:T(8,128)(2,1)}, bf16[1024,1024]{1,0:T(8,128)(2,1)}, u32[]{:S(2)}, u32[]{:S(2)}) collective-permute-start(bf16[1024,1024]{1,0:T(8,128)(2,1)} %refs_9_.3), channel_id=1, source_target_pairs={{0,1},{1,0},{2,3},{3,2},{4,5},{5,4},{6,7},{7,6},{8,9},{9,8},{10,11... | collective-permute-start | bytes 6291464 | tf_op jit(solution)/shard_map/ppermute | solution.py:843
  2.9 7.6 %collective-permute-start = (f32[8,1024]{1,0:T(8,128)S(1)}, f32[8,1024]{1,0:T(8,128)S(1)}, u32[]{:S(2)}, u32[]{:S(2)}) collective-permute-start(f32[8,1024]{1,0:T(8,128)S(1)} %dynamic_update_slice.3.refs_0_), channel_id=1, source_target_pairs={{0,1},{1,0},{2,3},{3,2},{4,5},{5,4},{6,7},{7,6},{8,9},{9,8},{10,11... | collective-permute-start | bytes 98312 | tf_op jit(solution)/shard_map/ppermute | solution.py:843
  5.4 13.5 %collective-permute-start.4 = (bf16[1,128,768]{2,1,0:T(8,128)(2,1)S(1)}, bf16[1,128,768]{2,1,0:T(8,128)(2,1)S(1)}, u32[]{:S(2)}, u32[]{:S(2)}) collective-permute-start(bf16[1,128,768]{2,1,0:T(8,128)(2,1)S(1)} %maximum_bitcast_fusion.refs_1_), channel_id=1, source_target_pairs={{0,16},{4,20},{8,24},{12,28},{16,0},{20,4},{24,8},{28,12},{1,17},{... | collective-permute-start | bytes 589832 | tf_op jit(solution)/shard_map/ppermute | solution.py:843
  9.1 17.2 %collective-permute-start.6 = (bf16[2,64,1024]{2,1,0:T(8,128)(2,1)}, bf16[2,64,1024]{2,1,0:T(8,128)(2,1)S(1)}, u32[]{:S(2)}, u32[]{:S(2)}) collective-permute-start(bf16[2,64,1024]{2,1,0:T(8,128)(2,1)} %refs_2_.1), channel_id=1, source_target_pairs={{0,2},{1,3},{2,0},{3,1},{4,6},{5,7},{6,4},{7,5},{8,10},{9,11},{10,... | collective-permute-start | bytes 786440 | tf_op jit(solution)/shard_map/ppermute | solution.py:843
  19.5 12.2 %collective-permute-start.5 = (bf16[2,128,768]{2,1,0:T(8,128)(2,1)S(1)}, bf16[2,128,768]{2,1,0:T(8,128)(2,1)S(1)}, u32[]{:S(2)}, u32[]{:S(2)}) collective-permute-start(bf16[2,128,768]{2,1,0:T(8,128)(2,1)S(1)} %bitcast.87), channel_id=1, source_target_pairs={{0,8},{4,12},{8,0},{12,4},{16,24},{20,28},{24,16},{28,20},{1,9},{5... | collective-permute-start | bytes 1179656 | tf_op jit(solution)/shard_map/ppermute | solution.py:843
  26.2 6.1 %collective-permute-start.3 = (f32[8,256]{1,0:T(8,128)S(1)}, f32[8,256]{1,0:T(8,128)S(1)}, u32[]{:S(2)}, u32[]{:S(2)}) collective-permute-start(f32[8,256]{1,0:T(8,128)S(1)} %pad_maximum_fusion.2), channel_id=1, source_target_pairs={{0,1},{1,0},{2,3},{3,2},{4,5},{5,4},{6,7},{7,6},{8,9},{9,8},{10,11... | collective-permute-start | bytes 24584 | tf_op jit(solution)/shard_map/ppermute | solution.py:843
  26.8 4.9 %collective-permute-start.8 = (f32[8,1024]{1,0:T(8,128)S(1)}, f32[8,1024]{1,0:T(8,128)S(1)}, u32[]{:S(2)}, u32[]{:S(2)}) collective-permute-start(f32[8,1024]{1,0:T(8,128)S(1)} %shard_map.404.refs_0_), channel_id=1, source_target_pairs={{0,16},{4,20},{8,24},{12,28},{16,0},{20,4},{24,8},{28,12},{1,17},{... | collective-permute-start | bytes 98312 | tf_op jit(solution)/shard_map/ppermute | solution.py:843
  32.3 11.6 %collective-permute-start.13 = (bf16[1024,768]{1,0:T(8,128)(2,1)S(1)}, bf16[1024,768]{1,0:T(8,128)(2,1)S(1)}, u32[]{:S(2)}, u32[]{:S(2)}) collective-permute-start(bf16[1024,768]{1,0:T(8,128)(2,1)S(1)} %pad_maximum_fusion.refs_7_.refs_8_), channel_id=1, source_target_pairs={{0,1},{1,0},{2,3},{3,2},{4,5},{5,4},{6,7},{7,6},{8,9},{9,8},{10,11... | collective-permute-start | bytes 4718600 | tf_op jit(solution)/shard_map/ppermute | solution.py:843
  32.9 27.9 %collective-permute-start.16 = (bf16[4,128,768]{2,1,0:T(8,128)(2,1)S(1)}, bf16[4,128,768]{2,1,0:T(8,128)(2,1)S(1)}, u32[]{:S(2)}, u32[]{:S(2)}) collective-permute-start(bf16[4,128,768]{2,1,0:T(8,128)(2,1)S(1)} %bitcast.79), channel_id=1, source_target_pairs={{0,4},{4,0},{8,12},{12,8},{16,20},{20,16},{24,28},{28,24},{1,5},{5... | collective-permute-start | bytes 2359304 | tf_op jit(solution)/shard_map/ppermute | solution.py:843
  42.3 14.2 %collective-permute-start.12 = (bf16[256,1024]{1,0:T(8,128)(2,1)S(1)}, bf16[256,1024]{1,0:T(8,128)(2,1)S(1)}, u32[]{:S(2)}, u32[]{:S(2)}) collective-permute-start(bf16[256,1024]{1,0:T(8,128)(2,1)S(1)} %get-tuple-element.327.refs_3_), channel_id=1, source_target_pairs={{0,2},{1,3},{2,0},{3,1},{4,6},{5,7},{6,4},{7,5},{8,10},{9,11},{10,... | collective-permute-start | bytes 1572872 | tf_op jit(solution)/shard_map/ppermute | solution.py:843
  61.4 14.9 %collective-permute-start.19 = (bf16[1024,768]{1,0:T(8,128)(2,1)S(1)}, bf16[1024,768]{1,0:T(8,128)(2,1)S(1)}, u32[]{:S(2)}, u32[]{:S(2)}) collective-permute-start(bf16[1024,768]{1,0:T(8,128)(2,1)S(1)} %bitcast.73), channel_id=1, source_target_pairs={{0,1},{1,0},{2,3},{3,2},{4,5},{5,4},{6,7},{7,6},{8,9},{9,8},{10,11... | collective-permute-start | bytes 4718600 | tf_op jit(solution)/shard_map/ppermute | solution.py:843
  62.1 14.3 %collective-permute-start.15 = (bf16[256,1024]{1,0:T(8,128)(2,1)S(1)}, bf16[256,1024]{1,0:T(8,128)(2,1)S(1)}, u32[]{:S(2)}, u32[]{:S(2)}) collective-permute-start(bf16[256,1024]{1,0:T(8,128)(2,1)S(1)} %get-tuple-element.332.refs_1_), channel_id=1, source_target_pairs={{0,2},{1,3},{2,0},{3,1},{4,6},{5,7},{6,4},{7,5},{8,10},{9,11},{10,... | collective-permute-start | bytes 1572872 | tf_op jit(solution)/shard_map/ppermute | solution.py:843
  79.9 27.2 %collective-permute-start.26 = (bf16[1024,1024]{1,0:T(8,128)(2,1)S(1)}, bf16[1024,1024]{1,0:T(8,128)(2,1)S(1)}, u32[]{:S(2)}, u32[]{:S(2)}) collective-permute-start(bf16[1024,1024]{1,0:T(8,128)(2,1)S(1)} %copy-done.9), channel_id=1, source_target_pairs={{0,1},{1,0},{2,3},{3,2},{4,5},{5,4},{6,7},{7,6},{8,9},{9,8},{10,11... | collective-permute-start | bytes 6291464 | tf_op jit(solution)/shard_map/ppermute | solution.py:843
  80.0 27.1 %collective-permute-start.27 = (bf16[1024,1024]{1,0:T(8,128)(2,1)S(1)}, bf16[1024,1024]{1,0:T(8,128)(2,1)S(1)}, u32[]{:S(2)}, u32[]{:S(2)}) collective-permute-start(bf16[1024,1024]{1,0:T(8,128)(2,1)S(1)} %copy-done.10), channel_id=1, source_target_pairs={{0,1},{1,0},{2,3},{3,2},{4,5},{5,4},{6,7},{7,6},{8,9},{9,8},{10,11... | collective-permute-start | bytes 6291464 | tf_op jit(solution)/shard_map/ppermute | solution.py:843
  80.5 11.0 %collective-permute-start.23 = (bf16[2,64,1024]{2,1,0:T(8,128)(2,1)S(1)}, bf16[2,64,1024]{2,1,0:T(8,128)(2,1)S(1)}, u32[]{:S(2)}, u32[]{:S(2)}) collective-permute-start(bf16[2,64,1024]{2,1,0:T(8,128)(2,1)S(1)} %copy-done.2), channel_id=1, source_target_pairs={{0,2},{1,3},{2,0},{3,1},{4,6},{5,7},{6,4},{7,5},{8,10},{9,11},{10,... | collective-permute-start | bytes 786440 | tf_op jit(solution)/shard_map/ppermute | solution.py:843
  96.2 11.0 %collective-permute-start.24 = (bf16[256,1024]{1,0:T(8,128)(2,1)S(1)}, bf16[256,1024]{1,0:T(8,128)(2,1)S(1)}, u32[]{:S(2)}, u32[]{:S(2)}) collective-permute-start(bf16[256,1024]{1,0:T(8,128)(2,1)S(1)} %get-tuple-element.350.refs_0_), channel_id=1, source_target_pairs={{0,2},{1,3},{2,0},{3,1},{4,6},{5,7},{6,4},{7,5},{8,10},{9,11},{10,... | collective-permute-start | bytes 1572872 | tf_op jit(solution)/shard_map/ppermute | solution.py:843
  97.4 15.0 %collective-permute-start.33 = (bf16[256,1024]{1,0:T(8,128)(2,1)S(1)}, bf16[256,1024]{1,0:T(8,128)(2,1)S(1)}, u32[]{:S(2)}, u32[]{:S(2)}) collective-permute-start(bf16[256,1024]{1,0:T(8,128)(2,1)S(1)} %get-tuple-element.368.refs_9_), channel_id=1, source_target_pairs={{0,1},{1,0},{2,3},{3,2},{4,5},{5,4},{6,7},{7,6},{8,9},{9,8},{10,11... | collective-permute-start | bytes 1572872 | tf_op jit(solution)/shard_map/ppermute | solution.py:843
  98.9 13.2 %collective-permute-start.34 = (bf16[256,256]{1,0:T(8,128)(2,1)S(1)}, bf16[256,256]{1,0:T(8,128)(2,1)S(1)}, u32[]{:S(2)}, u32[]{:S(2)}) collective-permute-start(bf16[256,256]{1,0:T(8,128)(2,1)S(1)} %get-tuple-element.369), channel_id=1, source_target_pairs={{0,1},{1,0},{2,3},{3,2},{4,5},{5,4},{6,7},{7,6},{8,9},{9,8},{10,11... | collective-permute-start | bytes 393224 | tf_op jit(solution)/shard_map/ppermute | solution.py:843
  112.1 14.3 %collective-permute-start.28 = (bf16[256,1024]{1,0:T(8,128)(2,1)S(1)}, bf16[256,1024]{1,0:T(8,128)(2,1)S(1)}, u32[]{:S(2)}, u32[]{:S(2)}) collective-permute-start(bf16[256,1024]{1,0:T(8,128)(2,1)S(1)} %get-tuple-element.358.refs_1_), channel_id=1, source_target_pairs={{0,2},{1,3},{2,0},{3,1},{4,6},{5,7},{6,4},{7,5},{8,10},{9,11},{10,... | collective-permute-start | bytes 1572872 | tf_op jit(solution)/shard_map/ppermute | solution.py:843
  132.6 13.9 %collective-permute-start.37 = (bf16[256,1024]{1,0:T(8,128)(2,1)S(1)}, bf16[256,1024]{1,0:T(8,128)(2,1)S(1)}, u32[]{:S(2)}, u32[]{:S(2)}) collective-permute-start(bf16[256,1024]{1,0:T(8,128)(2,1)S(1)} %get-tuple-element.384.refs_0_), channel_id=1, source_target_pairs={{0,2},{1,3},{2,0},{3,1},{4,6},{5,7},{6,4},{7,5},{8,10},{9,11},{10,... | collective-permute-start | bytes 1572872 | tf_op jit(solution)/shard_map/ppermute | solution.py:843
  148.7 13.0 %collective-permute-start.42 = (bf16[256,1024]{1,0:T(8,128)(2,1)S(1)}, bf16[256,1024]{1,0:T(8,128)(2,1)S(1)}, u32[]{:S(2)}, u32[]{:S(2)}) collective-permute-start(bf16[256,1024]{1,0:T(8,128)(2,1)S(1)} %get-tuple-element.394.refs_10_.refs_5_), channel_id=1, source_target_pairs={{0,1},{1,0},{2,3},{3,2},{4,5},{5,4},{6,7},{7,6},{8,9},{9,8},{10,11... | collective-permute-start | bytes 1572872 | tf_op jit(solution)/shard_map/ppermute | solution.py:843
  148.8 13.0 %collective-permute-start.41 = (bf16[64,1024]{1,0:T(8,128)(2,1)S(1)}, bf16[64,1024]{1,0:T(8,128)(2,1)S(1)}, u32[]{:S(2)}, u32[]{:S(2)}) collective-permute-start(bf16[64,1024]{1,0:T(8,128)(2,1)S(1)} %get-tuple-element.393), channel_id=1, source_target_pairs={{0,1},{1,0},{2,3},{3,2},{4,5},{5,4},{6,7},{7,6},{8,9},{9,8},{10,11... | collective-permute-start | bytes 393224 | tf_op jit(solution)/shard_map/ppermute | solution.py:843
  156.8 5.0 %collective-permute-start.40 = (f32[8,512]{1,0:T(8,128)S(1)}, f32[8,512]{1,0:T(8,128)S(1)}, u32[]{:S(2)}, u32[]{:S(2)}) collective-permute-start(f32[8,512]{1,0:T(8,128)S(1)} %shard_map.421.refs_1_), channel_id=1, source_target_pairs={{0,16},{4,20},{8,24},{12,28},{16,0},{20,4},{24,8},{28,12},{1,17},{... | collective-permute-start | bytes 49160 | tf_op jit(solution)/shard_map/ppermute | solution.py:843
  158.5 22.6 %collective-permute-start.47 = (bf16[4,128,1024]{2,1,0:T(8,128)(2,1)S(1)}, bf16[4,128,1024]{2,1,0:T(8,128)(2,1)S(1)}, u32[]{:S(2)}, u32[]{:S(2)}) collective-permute-start(bf16[4,128,1024]{2,1,0:T(8,128)(2,1)S(1)} %get-tuple-element.420), channel_id=1, source_target_pairs={{0,4},{4,0},{8,12},{12,8},{16,20},{20,16},{24,28},{28,24},{1,5},{5... | collective-permute-start | bytes 3145736 | tf_op jit(solution)/shard_map/ppermute | solution.py:843
  160.0 22.5 %collective-permute-start.46 = (bf16[4,128,1024]{2,1,0:T(8,128)(2,1)S(1)}, bf16[4,128,1024]{2,1,0:T(8,128)(2,1)S(1)}, u32[]{:S(2)}, u32[]{:S(2)}) collective-permute-start(bf16[4,128,1024]{2,1,0:T(8,128)(2,1)S(1)} %get-tuple-element.418), channel_id=1, source_target_pairs={{0,8},{4,12},{8,0},{12,4},{16,24},{20,28},{24,16},{28,20},{1,9},{5... | collective-permute-start | bytes 3145736 | tf_op jit(solution)/shard_map/ppermute | solution.py:843
  164.5 10.8 %collective-permute-start.43 = (bf16[256,1024]{1,0:T(8,128)(2,1)S(1)}, bf16[256,1024]{1,0:T(8,128)(2,1)S(1)}, u32[]{:S(2)}, u32[]{:S(2)}) collective-permute-start(bf16[256,1024]{1,0:T(8,128)(2,1)S(1)} %get-tuple-element.400.refs_0_), channel_id=1, source_target_pairs={{0,2},{1,3},{2,0},{3,1},{4,6},{5,7},{6,4},{7,5},{8,10},{9,11},{10,... | collective-permute-start | bytes 1572872 | tf_op jit(solution)/shard_map/ppermute | solution.py:843
  186.6 51.4 %collective-permute-start.56 = (bf16[4,128,1792]{2,1,0:T(8,128)(2,1)S(1)}, bf16[4,128,1792]{2,1,0:T(8,128)(2,1)S(1)}, u32[]{:S(2)}, u32[]{:S(2)}) collective-permute-start(bf16[4,128,1792]{2,1,0:T(8,128)(2,1)S(1)} %get-tuple-element.477), channel_id=1, source_target_pairs={{0,4},{4,0},{8,12},{12,8},{16,20},{20,16},{24,28},{28,24},{1,5},{5... | collective-permute-start | bytes 5505032 | tf_op jit(solution)/shard_map/ppermute | solution.py:843
  187.5 12.6 %collective-permute-start.45 = (bf16[256,1024]{1,0:T(8,128)(2,1)S(1)}, bf16[256,1024]{1,0:T(8,128)(2,1)S(1)}, u32[]{:S(2)}, u32[]{:S(2)}) collective-permute-start(bf16[256,1024]{1,0:T(8,128)(2,1)S(1)} %get-tuple-element.407.refs_1_), channel_id=1, source_target_pairs={{0,2},{1,3},{2,0},{3,1},{4,6},{5,7},{6,4},{7,5},{8,10},{9,11},{10,... | collective-permute-start | bytes 1572872 | tf_op jit(solution)/shard_map/ppermute | solution.py:843
  187.8 22.4 %collective-permute-start.52 = (bf16[2,128,1024]{2,1,0:T(8,128)(2,1)S(1)}, bf16[2,128,1024]{2,1,0:T(8,128)(2,1)S(1)}, u32[]{:S(2)}, u32[]{:S(2)}) collective-permute-start(bf16[2,128,1024]{2,1,0:T(8,128)(2,1)S(1)} %get-tuple-element.447), channel_id=1, source_target_pairs={{0,8},{4,12},{8,0},{12,4},{16,24},{20,28},{24,16},{28,20},{1,9},{5... | collective-permute-start | bytes 1572872 | tf_op jit(solution)/shard_map/ppermute | solution.py:843
  189.5 24.2 %collective-permute-start.51 = (bf16[1,256,1024]{2,1,0:T(8,128)(2,1)S(1)}, bf16[1,256,1024]{2,1,0:T(8,128)(2,1)S(1)}, u32[]{:S(2)}, u32[]{:S(2)}) collective-permute-start(bf16[1,256,1024]{2,1,0:T(8,128)(2,1)S(1)} %get-tuple-element.445), channel_id=1, source_target_pairs={{0,16},{4,20},{8,24},{12,28},{16,0},{20,4},{24,8},{28,12},{1,17},{... | collective-permute-start | bytes 1572872 | tf_op jit(solution)/shard_map/ppermute | solution.py:843
  206.9 8.3 %collective-permute-start.53 = (bf16[256,1024]{1,0:T(8,128)(2,1)S(1)}, bf16[256,1024]{1,0:T(8,128)(2,1)S(1)}, u32[]{:S(2)}, u32[]{:S(2)}) collective-permute-start(bf16[256,1024]{1,0:T(8,128)(2,1)S(1)} %get-tuple-element.465), channel_id=1, source_target_pairs={{0,1},{1,0},{2,3},{3,2},{4,5},{5,4},{6,7},{7,6},{8,9},{9,8},{10,11... | collective-permute-start | bytes 1572872 | tf_op jit(solution)/shard_map/ppermute | solution.py:843
  206.9 10.9 %collective-permute-start.50 = (bf16[256,1024]{1,0:T(8,128)(2,1)S(1)}, bf16[256,1024]{1,0:T(8,128)(2,1)S(1)}, u32[]{:S(2)}, u32[]{:S(2)}) collective-permute-start(bf16[256,1024]{1,0:T(8,128)(2,1)S(1)} %get-tuple-element.441.refs_1_), channel_id=1, source_target_pairs={{0,1},{1,0},{2,3},{3,2},{4,5},{5,4},{6,7},{7,6},{8,9},{9,8},{10,11... | collective-permute-start | bytes 1572872 | tf_op jit(solution)/shard_map/ppermute | solution.py:843
  210.2 10.0 %collective-permute-start.58 = (bf16[128,1024]{1,0:T(8,128)(2,1)S(1)}, bf16[128,1024]{1,0:T(8,128)(2,1)S(1)}, u32[]{:S(2)}, u32[]{:S(2)}) collective-permute-start(bf16[128,1024]{1,0:T(8,128)(2,1)S(1)} %get-tuple-element.483), channel_id=1, source_target_pairs={{0,2},{1,3},{2,0},{3,1},{4,6},{5,7},{6,4},{7,5},{8,10},{9,11},{10,... | collective-permute-start | bytes 786440 | tf_op jit(solution)/shard_map/ppermute | solution.py:843
  213.7 23.7 %collective-permute-start.57 = (bf16[1,128,1024]{2,1,0:T(8,128)(2,1)S(1)}, bf16[1,128,1024]{2,1,0:T(8,128)(2,1)S(1)}, u32[]{:S(2)}, u32[]{:S(2)}) collective-permute-start(bf16[1,128,1024]{2,1,0:T(8,128)(2,1)S(1)} %get-tuple-element.479), channel_id=1, source_target_pairs={{0,16},{4,20},{8,24},{12,28},{16,0},{20,4},{24,8},{28,12},{1,17},{... | collective-permute-start | bytes 786440 | tf_op jit(solution)/shard_map/ppermute | solution.py:843
  217.4 44.3 %collective-permute-start.55 = (bf16[4,128,1024]{2,1,0:T(8,128)(2,1)S(1)}, bf16[4,128,1024]{2,1,0:T(8,128)(2,1)S(1)}, u32[]{:S(2)}, u32[]{:S(2)}) collective-permute-start(bf16[4,128,1024]{2,1,0:T(8,128)(2,1)S(1)} %get-tuple-element.475), channel_id=1, source_target_pairs={{0,4},{4,0},{8,12},{12,8},{16,20},{20,16},{24,28},{28,24},{1,5},{5... | collective-permute-start | bytes 3145736 | tf_op jit(solution)/shard_map/ppermute | solution.py:843
  224.2 9.2 %collective-permute-start.60 = (f32[8,1024]{1,0:T(8,128)S(1)}, f32[8,1024]{1,0:T(8,128)S(1)}, u32[]{:S(2)}, u32[]{:S(2)}) collective-permute-start(f32[8,1024]{1,0:T(8,128)S(1)} %slice.74.refs_0_), channel_id=1, source_target_pairs={{0,2},{1,3},{2,0},{3,1},{4,6},{5,7},{6,4},{7,5},{8,10},{9,11},{10,... | collective-permute-start | bytes 98312 | tf_op jit(solution)/shard_map/ppermute | solution.py:843
  239.0 21.9 %collective-permute-start.62 = (bf16[2,128,1792]{2,1,0:T(8,128)(2,1)S(1)}, bf16[2,128,1792]{2,1,0:T(8,128)(2,1)S(1)}, u32[]{:S(2)}, u32[]{:S(2)}) collective-permute-start(bf16[2,128,1792]{2,1,0:T(8,128)(2,1)S(1)} %get-tuple-element.508), channel_id=1, source_target_pairs={{0,8},{4,12},{8,0},{12,4},{16,24},{20,28},{24,16},{28,20},{1,9},{5... | collective-permute-start | bytes 2752520 | tf_op jit(solution)/shard_map/ppermute | solution.py:843
  239.0 33.5 %collective-permute-start.54 = (bf16[4,128,1024]{2,1,0:T(8,128)(2,1)S(1)}, bf16[4,128,1024]{2,1,0:T(8,128)(2,1)S(1)}, u32[]{:S(2)}, u32[]{:S(2)}) collective-permute-start(bf16[4,128,1024]{2,1,0:T(8,128)(2,1)S(1)} %get-tuple-element.473), channel_id=1, source_target_pairs={{0,4},{4,0},{8,12},{12,8},{16,20},{20,16},{24,28},{28,24},{1,5},{5... | collective-permute-start | bytes 3145736 | tf_op jit(solution)/shard_map/ppermute | solution.py:843
  241.1 17.6 %collective-permute-start.63 = (f32[8,1280]{1,0:T(8,128)S(1)}, f32[8,1280]{1,0:T(8,128)S(1)}, u32[]{:S(2)}, u32[]{:S(2)}) collective-permute-start(f32[8,1280]{1,0:T(8,128)S(1)} %shard_map.438.refs_0_), channel_id=1, source_target_pairs={{0,16},{4,20},{8,24},{12,28},{16,0},{20,4},{24,8},{28,12},{1,17},{... | collective-permute-start | bytes 122888 | tf_op jit(solution)/shard_map/ppermute | solution.py:843
  262.4 22.1 %collective-permute-start.66 = (bf16[2,128,1024]{2,1,0:T(8,128)(2,1)S(1)}, bf16[2,128,1024]{2,1,0:T(8,128)(2,1)S(1)}, u32[]{:S(2)}, u32[]{:S(2)}) collective-permute-start(bf16[2,128,1024]{2,1,0:T(8,128)(2,1)S(1)} %get-tuple-element.537), channel_id=1, source_target_pairs={{0,8},{4,12},{8,0},{12,4},{16,24},{20,28},{24,16},{28,20},{1,9},{5... | collective-permute-start | bytes 1572872 | tf_op jit(solution)/shard_map/ppermute | solution.py:843
  265.4 23.3 %collective-permute-start.65 = (bf16[1,128,1792]{2,1,0:T(8,128)(2,1)S(1)}, bf16[1,128,1792]{2,1,0:T(8,128)(2,1)S(1)}, u32[]{:S(2)}, u32[]{:S(2)}) collective-permute-start(bf16[1,128,1792]{2,1,0:T(8,128)(2,1)S(1)} %get-tuple-element.535), channel_id=1, source_target_pairs={{0,16},{4,20},{8,24},{12,28},{16,0},{20,4},{24,8},{28,12},{1,17},{... | collective-permute-start | bytes 1376264 | tf_op jit(solution)/shard_map/ppermute | solution.py:843
  265.6 26.8 %collective-permute-start.70 = (f32[64,1024]{1,0:T(8,128)}, f32[64,1024]{1,0:T(8,128)}, u32[]{:S(2)}, u32[]{:S(2)}) collective-permute-start(f32[64,1024]{1,0:T(8,128)} %get-tuple-element.570), channel_id=1, source_target_pairs={{0,1},{1,0},{2,3},{3,2},{4,5},{5,4},{6,7},{7,6},{8,9},{9,8},{10,11... | collective-permute-start | bytes 786440 | tf_op jit(solution)/shard_map/ppermute | solution.py:843
  285.8 12.7 %collective-permute-start.68 = (bf16[1,128,1024]{2,1,0:T(8,128)(2,1)}, bf16[1,128,1024]{2,1,0:T(8,128)(2,1)}, u32[]{:S(2)}, u32[]{:S(2)}) collective-permute-start(bf16[1,128,1024]{2,1,0:T(8,128)(2,1)} %get-tuple-element.556), channel_id=1, source_target_pairs={{0,16},{4,20},{8,24},{12,28},{16,0},{20,4},{24,8},{28,12},{1,17},{... | collective-permute-start | bytes 786440 | tf_op jit(solution)/shard_map/ppermute | solution.py:843
  286.2 18.0 %collective-permute-start.64 = (bf16[2,128,1024]{2,1,0:T(8,128)(2,1)}, bf16[2,128,1024]{2,1,0:T(8,128)(2,1)}, u32[]{:S(2)}, u32[]{:S(2)}) collective-permute-start(bf16[2,128,1024]{2,1,0:T(8,128)(2,1)} %get-tuple-element.532), channel_id=1, source_target_pairs={{0,8},{4,12},{8,0},{12,4},{16,24},{20,28},{24,16},{28,20},{1,9},{5... | collective-permute-start | bytes 1572872 | tf_op jit(solution)/shard_map/ppermute | solution.py:843
  289.5 10.0 %collective-permute-start.67 = (f32[8,1280]{1,0:T(8,128)S(1)}, f32[8,1280]{1,0:T(8,128)S(1)}, u32[]{:S(2)}, u32[]{:S(2)}) collective-permute-start(f32[8,1280]{1,0:T(8,128)S(1)} %shard_map.441.refs_0_), channel_id=1, source_target_pairs={{0,4},{4,0},{8,12},{12,8},{16,20},{20,16},{24,28},{28,24},{1,5},{5... | collective-permute-start | bytes 122888 | tf_op jit(solution)/shard_map/ppermute | solution.py:843
  291.6 15.7 %collective-permute-start.71 = (bf16[1,128,1024]{2,1,0:T(8,128)(2,1)}, bf16[1,128,1024]{2,1,0:T(8,128)(2,1)S(1)}, u32[]{:S(2)}, u32[]{:S(2)}) collective-permute-start(bf16[1,128,1024]{2,1,0:T(8,128)(2,1)} %copy-done.7), channel_id=1, source_target_pairs={{0,4},{4,0},{8,12},{12,8},{16,20},{20,16},{24,28},{28,24},{1,5},{5... | collective-permute-start | bytes 786440 | tf_op jit(solution)/shard_map/ppermute | solution.py:843
  305.4 12.6 %collective-permute-start.69 = (bf16[1,128,1024]{2,1,0:T(8,128)(2,1)S(1)}, bf16[1,128,1024]{2,1,0:T(8,128)(2,1)S(1)}, u32[]{:S(2)}, u32[]{:S(2)}) collective-permute-start(bf16[1,128,1024]{2,1,0:T(8,128)(2,1)S(1)} %get-tuple-element.568), channel_id=1, source_target_pairs={{0,16},{4,20},{8,24},{12,28},{16,0},{20,4},{24,8},{28,12},{1,17},{... | collective-permute-start | bytes 786440 | tf_op jit(solution)/shard_map/ppermute | solution.py:843
  (44 other events, 238.4 us)
where the time goes:
time: 321 us; the launch traced here: 320 us
  waiting for transfers between devices  154 us (48%)
  Pallas kernels  73.1 us (23%)
  starting transfers between devices  71.4 us (22%)
  local copies, waits for them, and re-layouts  17 us (5%)
    ppermute x72, waiting for transfers between devices, swap(): lax.ppermute(value, axis, [(place, place ^ bit) for place in range(size)])  154 us
    pallas_call x54, Pallas kernels, run(): pl.pallas_call(body if many else plain, out_shape=[pltpu.HBM(shape, kind)...  73.1 us
    ppermute x72, starting transfers between devices, swap(): lax.ppermute(value, axis, [(place, place ^ bit) for place in range(size)])  71.4 us
    unnamed x54, local copies, waits for them, and re-layouts  12.3 us
  transfers between devices with their start and end apart: 72, of which 37 were waited for; matrix products, arithmetic and copies ran while one was open for 5% of the time, Pallas kernels for 18%

commit v1 on v0

--- a/solution.py
+++ b/solution.py
@@ -1306,6 +1306,9 @@
         scratch=[((span, width), F32)],
     )
     frames_other = beside(frames_sent)
+    chain = Chain(last_sums)
+    middle.step(chain)
+    last_sums = chain.last
     (smalls,) = run(
         k_smalls, [((8, width + 2 * channels), F32)],
         [last_sums, sum_attn, sum_conv, sum_two, sum_final, small_sums], scalars=0,
@@ -1333,15 +1336,12 @@
         return total
 
     first, *between = [1 << level for level in range(1, lax.axis_size("dp").bit_length() - 1)]
-    gains = add(*hop(gains, first))
-    gains, chain.last = tie(gains, chain.last)
     (two_up,) = two_up.finish(chain, ((block, hidden_width), False))
     middle.step(chain)
-    for bit in between:
+    one_up.step(chain)
+    for bit in [first, *between]:
         gains = add(*hop(gains, bit))
     gains, chain.last = tie(gains, chain.last)
-    middle.step(chain)
-    one_up.step(chain)
     one_down.step(chain)
     one_up.step(chain)
     conv_up_grad, conv_down_grad, query_grad, key_grad, value_grad, output_grad = middle.finish(

time: 321 us -> 319 us (level)
  starting transfers between devices: 71.4 us -> 65.7 us
  waiting for transfers between devices: 154 us -> 158 us
    ppermute x72, starting transfers between devices: 71.4 us -> 65.7 us  [swap(): lax.ppermute(value, axis, [(place, place ^ bit) for place in range(size)])]
    ppermute x72, waiting for transfers between devices: 154 us -> 158 us  [swap(): lax.ppermute(value, axis, [(place, place ^ bit) for place in range(size)])]
  transfers between devices with their start and end apart: 72 -> 72, of which waited for: 37 -> 36; matrix products, arithmetic and copies ran while one was open for 5% -> 5% of each run, Pallas kernels for 18% -> 18%
where the time goes in v1:
time: 319 us; the launch traced here: 318 us
  waiting for transfers between devices  158 us (50%)
  Pallas kernels  73.2 us (23%)
  starting transfers between devices  65.7 us (21%)
  local copies, waits for them, and re-layouts  16.3 us (5%)
    ppermute x72, waiting for transfers between devices, swap(): lax.ppermute(value, axis, [(place, place ^ bit) for place in range(size)])  158 us
    pallas_call x54, Pallas kernels, run(): pl.pallas_call(body if many else plain, out_shape=[pltpu.HBM(shape, kind)...  73.2 us
    ppermute x72, starting transfers between devices, swap(): lax.ppermute(value, axis, [(place, place ^ bit) for place in range(size)])  65.7 us
    unnamed x54, local copies, waits for them, and re-layouts  11.6 us
  transfers between devices with their start and end apart: 72, of which 36 were waited for; matrix products, arithmetic and copies ran while one was open for 5% of the time, Pallas kernels for 18%

profile of v1, /device:TPU:0, one launch (start us, length us, event | category | flops | bytes accessed | tf_op | source)
XLA Modules:
  0.0 318.4 jit_solution(11223874468141749271)
XLA Ops:
  5.4 3.7 %collective-permute-start.4 = (bf16[1,128,768]{2,1,0:T(8,128)(2,1)S(1)}, bf16[1,128,768]{2,1,0:T(8,128)(2,1)S(1)}, u32[]{:S(2)}, u32[]{:S(2)}) collective-permute-start(bf16[1,128,768]{2,1,0:T(8,128)(2,1)S(1)} %maximum_bitcast_fusion.refs_1_), channel_id=1, source_target_pairs={{0,16},{4,20},{8,24},{12,28},{16,0},{20,4},{24,8},{28,12},{1,17},{... | collective-permute-start | bytes 589832 | tf_op jit(solution)/shard_map/ppermute | solution.py:843
  16.5 2.4 collective-permute-done.2.refs_1_
  19.5 2.2 collective-permute-start.5
  26.8 2.0 collective-permute-start.8
  28.9 2.8 collective-permute-done.8.refs_1_
  36.2 5.9 %shard_map.407 = (bf16[256,1024]{1,0:T(8,128)(2,1)S(1)}, bf16[256,1024]{1,0:T(8,128)(2,1)S(1)}, bf16[256,1024]{1,0:T(8,128)(2,1)S(1)}, bf16[256,1024]{1,0:T(8,12...) custom-call(s32[4]{0:T(128)S(1)} %pad_add_fusion.refs_0_, ...), custom_call_target="tpu_custom_call" | custom-call | flops 1 | bytes 1 | tf_op jit(solution)/shard_map/pallas_call | solution.py:822
  44.1 12.4 %collective-permute-done.12.refs_4_ = bf16[256,1024]{1,0:T(8,128)(2,1)S(1)} collective-permute-done((bf16[256,1024]{1,0:T(8,128)(2,1)S(1)}, bf16[256,1024]{1,0:T(8,128)(2,1)S(1)}, u32[]{:S(2)}, u32[]{:S(2)}) %collective-permute-start.12) | collective-permute-done | bytes 524320 | tf_op jit(solution)/shard_map/ppermute | solution.py:843
  56.5 4.2 %shard_map.408 = (f32[256,1024]{1,0:T(8,128)S(1)}, bf16[256,1024]{1,0:T(8,128)(2,1)S(1)}, bf16[256,256]{1,0:T(8,128)(2,1)S(1)}, bf16[256,256]{1,0:T(8,128)(2,1)S...) custom-call(s32[4]{0:T(128)S(1)} %pad_add_fusion.refs_0_, ...), custom_call_target="tpu_custom_call" | custom-call | flops 1 | bytes 1 | tf_op jit(solution)/shard_map/pallas_call | solution.py:822
  63.6 2.0 collective-permute-done.18.refs_4_
  66.4 10.0 %collective-permute-done.15.refs_2_ = bf16[256,1024]{1,0:T(8,128)(2,1)S(1)} collective-permute-done((bf16[256,1024]{1,0:T(8,128)(2,1)S(1)}, bf16[256,1024]{1,0:T(8,128)(2,1)S(1)}, u32[]{:S(2)}, u32[]{:S(2)}) %collective-permute-start.15) | collective-permute-done | bytes 524320 | tf_op jit(solution)/shard_map/ppermute | solution.py:843
  76.4 3.5 %shard_map.410 = (f32[256,1024]{1,0:T(8,128)S(1)}, bf16[256,1024]{1,0:T(8,128)(2,1)S(1)}, f32[256,512]{1,0:T(8,128)S(1)}, f32[256,512]{1,0:T(8,128)S(1)}, f32[27...) custom-call(s32[4]{0:T(128)S(1)} %pad_add_fusion.refs_0_, ...), custom_call_target="tpu_custom_call" | custom-call | flops 1 | bytes 1 | tf_op jit(solution)/shard_map/pallas_call | solution.py:822
  83.5 2.2 collective-permute-done.20.refs_1_
  85.7 1.9 collective-permute-start.21
  87.7 1.9 collective-permute-done.21.refs_1_
  89.5 2.0 collective-permute-start.22
  91.5 2.7 collective-permute-done.22.refs_1_
  94.2 1.9 shard_map.413
  99.0 8.1 %collective-permute-done.24.refs_1_ = bf16[256,1024]{1,0:T(8,128)(2,1)S(1)} collective-permute-done((bf16[256,1024]{1,0:T(8,128)(2,1)S(1)}, bf16[256,1024]{1,0:T(8,128)(2,1)S(1)}, u32[]{:S(2)}, u32[]{:S(2)}) %collective-permute-start.24) | collective-permute-done | bytes 524320 | tf_op jit(solution)/shard_map/ppermute | solution.py:843
  107.1 4.3 %shard_map.415 = (f32[256,1024]{1,0:T(8,128)S(1)}, bf16[256,1024]{1,0:T(8,128)(2,1)S(1)}, bf16[256,1024]{1,0:T(8,128)(2,1)S(1)}, bf16[256,1024]{1,0:T(8,128)(2,1...) custom-call(bf16[256,1024]{1,0:T(8,128)(2,1)S(1)} %get-tuple-element.348.refs_0_, ...), custom_call_target="tpu_custom_call" | custom-call | flops 1 | bytes 1 | tf_op jit(solution)/shard_map/pallas_call | solution.py:822
  112.6 2.5 collective-permute-done.32.refs_8_
  115.1 11.3 %collective-permute-done.28.refs_2_ = bf16[256,1024]{1,0:T(8,128)(2,1)S(1)} collective-permute-done((bf16[256,1024]{1,0:T(8,128)(2,1)S(1)}, bf16[256,1024]{1,0:T(8,128)(2,1)S(1)}, u32[]{:S(2)}, u32[]{:S(2)}) %collective-permute-start.28) | collective-permute-done | bytes 524320 | tf_op jit(solution)/shard_map/ppermute | solution.py:843
  126.4 5.6 %shard_map.416 = (bf16[64,1024]{1,0:T(8,128)(2,1)S(1)}, bf16[64,1024]{1,0:T(8,128)(2,1)S(1)}, f32[256,1024]{1,0:T(8,128)S(1)}, f32[1,1024]{1,0:T(1,128)S(1)}, bf...) custom-call(s32[4]{0:T(128)S(1)} %pad_add_fusion.refs_0_, ...), custom_call_target="tpu_custom_call" | custom-call | flops 1 | bytes 1 | tf_op jit(solution)/shard_map/pallas_call | solution.py:822
  133.9 2.2 shard_map.418
  136.1 2.2 shard_map.417
  138.3 8.2 %collective-permute-done.37.refs_1_ = bf16[256,1024]{1,0:T(8,128)(2,1)S(1)} collective-permute-done((bf16[256,1024]{1,0:T(8,128)(2,1)S(1)}, bf16[256,1024]{1,0:T(8,128)(2,1)S(1)}, u32[]{:S(2)}, u32[]{:S(2)}) %collective-permute-start.37) | collective-permute-done | bytes 524320 | tf_op jit(solution)/shard_map/ppermute | solution.py:843
  146.4 2.2 shard_map.419
  150.8 2.2 collective-permute-done.38.refs_1_
  154.7 2.0 collective-permute-done.39.refs_1_
  161.7 2.7 shard_map.422
  166.3 8.9 %collective-permute-done.43.refs_1_ = bf16[256,1024]{1,0:T(8,128)(2,1)S(1)} collective-permute-done((bf16[256,1024]{1,0:T(8,128)(2,1)S(1)}, bf16[256,1024]{1,0:T(8,128)(2,1)S(1)}, u32[]{:S(2)}, u32[]{:S(2)}) %collective-permute-start.43) | collective-permute-done | bytes 524320 | tf_op jit(solution)/shard_map/ppermute | solution.py:843
  175.3 4.3 %shard_map.423 = (f32[256,1024]{1,0:T(8,128)S(1)}, f32[1,1024]{1,0:T(1,128)S(1)}, bf16[256,1024]{1,0:T(8,128)(2,1)S(1)}, bf16[256,768]{1,0:T(8,128)(2,1)S(1)}, b...) custom-call(bf16[256,1024]{1,0:T(8,128)(2,1)S(1)} %get-tuple-element.398.refs_0_, ...), custom_call_target="tpu_custom_call" | custom-call | flops 1 | bytes 1 | tf_op jit(solution)/shard_map/pallas_call | solution.py:822
  183.3 3.3 %shard_map.426 = (f32[4,128,1792]{2,1,0:T(8,128)S(1)}, bf16[4,128,1792]{2,1,0:T(8,128)(2,1)S(1)}) custom-call(s32[4]{0:T(128)S(1)} %pad_add_fusion.refs_0_, bf16[256,1024]{1,0:T(8,128)(2,1)S(1)} %get-tuple-element.364.refs_4_.refs_1_, bf16[256,1024]{1,0:T(8,128)(2,1)S(1)} %collective-permute-done.31.refs_2_, ...), custom_call_target="tpu_custom_call" | custom-call | flops 1 | bytes 1 | tf_op jit(solution)/shard_map/pallas_call | solution.py:822
  190.7 9.4 %collective-permute-done.45.refs_2_ = bf16[256,1024]{1,0:T(8,128)(2,1)S(1)} collective-permute-done((bf16[256,1024]{1,0:T(8,128)(2,1)S(1)}, bf16[256,1024]{1,0:T(8,128)(2,1)S(1)}, u32[]{:S(2)}, u32[]{:S(2)}) %collective-permute-start.45) | collective-permute-done | bytes 524320 | tf_op jit(solution)/shard_map/ppermute | solution.py:843
  200.0 6.8 %shard_map.427 = (f32[256,1024]{1,0:T(8,128)S(1)}, f32[1,1024]{1,0:T(1,128)S(1)}, bf16[256,1024]{1,0:T(8,128)(2,1)S(1)}, bf16[256,1024]{1,0:T(8,128)(2,1)S(1)}, ...) custom-call(s32[4]{0:T(128)S(1)} %pad_add_fusion.refs_0_, ...), custom_call_target="tpu_custom_call" | custom-call | flops 1 | bytes 1 | tf_op jit(solution)/shard_map/pallas_call | solution.py:822
  207.4 2.8 collective-permute-done.52
  214.4 2.2 shard_map.431
  217.1 2.4 shard_map.430
  219.6 1.9 shard_map.432
  221.5 8.1 %collective-permute-done.55 = bf16[4,128,1792]{2,1,0:T(8,128)(2,1)S(1)} collective-permute-done((bf16[4,128,1792]{2,1,0:T(8,128)(2,1)S(1)}, bf16[4,128,1792]{2,1,0:T(8,128)(2,1)S(1)}, u32[]{:S(2)}, u32[]{:S(2)}) %collective-permute-start.55) | collective-permute-done | bytes 1835040 | tf_op jit(solution)/shard_map/ppermute | solution.py:843
  234.9 17.6 %collective-permute-done.61 = bf16[1,128,1024]{2,1,0:T(8,128)(2,1)S(1)} collective-permute-done((bf16[1,128,1024]{2,1,0:T(8,128)(2,1)S(1)}, bf16[1,128,1024]{2,1,0:T(8,128)(2,1)S(1)}, u32[]{:S(2)}, u32[]{:S(2)}) %collective-permute-start.61) | collective-permute-done | bytes 262176 | tf_op jit(solution)/shard_map/ppermute | solution.py:843
  256.0 1.9 collective-permute-start.66
  260.5 3.6 %collective-permute-done.58.refs_1_ = f32[8,1024]{1,0:T(8,128)S(1)} collective-permute-done((f32[8,1024]{1,0:T(8,128)S(1)}, f32[8,1024]{1,0:T(8,128)S(1)}, u32[]{:S(2)}, u32[]{:S(2)}) %collective-permute-start.58) | collective-permute-done | bytes 32800 | tf_op jit(solution)/shard_map/ppermute | solution.py:843
  265.4 12.2 %collective-permute-done.62.refs_1_ = f32[8,1280]{1,0:T(8,128)S(1)} collective-permute-done((f32[8,1280]{1,0:T(8,128)S(1)}, f32[8,1280]{1,0:T(8,128)S(1)}, u32[]{:S(2)}, u32[]{:S(2)}) %collective-permute-start.62) | collective-permute-done | bytes 40992 | tf_op jit(solution)/shard_map/ppermute | solution.py:843
  278.7 4.0 %collective-permute-done.63.refs_1_ = f32[8,1280]{1,0:T(8,128)S(1)} collective-permute-done((f32[8,1280]{1,0:T(8,128)S(1)}, f32[8,1280]{1,0:T(8,128)S(1)}, u32[]{:S(2)}, u32[]{:S(2)}) %collective-permute-start.63) | collective-permute-done | bytes 40992 | tf_op jit(solution)/shard_map/ppermute | solution.py:843
  286.4 1.9 collective-permute-start.64
  289.1 4.1 %collective-permute-start.67 = (f32[8,1280]{1,0:T(8,128)S(1)}, f32[8,1280]{1,0:T(8,128)S(1)}, u32[]{:S(2)}, u32[]{:S(2)}) collective-permute-start(f32[8,1280]{1,0:T(8,128)S(1)} %shard_map.443.refs_0_), channel_id=1, source_target_pairs={{0,4},{4,0},{8,12},{12,8},{16,20},{20,16},{24,28},{28,24},{1,5},{5... | collective-permute-start | bytes 122888 | tf_op jit(solution)/shard_map/ppermute | solution.py:843
  301.7 2.0 collective-permute-done.64
  310.5 5.7 %collective-permute-done.69 = bf16[1,128,1024]{2,1,0:T(8,128)(2,1)S(1)} collective-permute-done((bf16[1,128,1024]{2,1,0:T(8,128)(2,1)S(1)}, bf16[1,128,1024]{2,1,0:T(8,128)(2,1)S(1)}, u32[]{:S(2)}, u32[]{:S(2)}) %collective-permute-start.69) | collective-permute-done | bytes 262176 | tf_op jit(solution)/shard_map/ppermute | solution.py:843
  (226 shorter events, 95.7 us)
Async XLA Ops:
  0.7 35.5 %collective-permute-start.10 = (bf16[1024,1024]{1,0:T(8,128)(2,1)}, bf16[1024,1024]{1,0:T(8,128)(2,1)S(1)}, u32[]{:S(2)}, u32[]{:S(2)}) collective-permute-start(bf16[1024,1024]{1,0:T(8,128)(2,1)} %refs_7_.1), channel_id=1, source_target_pairs={{0,1},{1,0},{2,3},{3,2},{4,5},{5,4},{6,7},{7,6},{8,9},{9,8},{10,11... | collective-permute-start | bytes 6291464 | tf_op jit(solution)/shard_map/ppermute | solution.py:843
  1.2 35.0 %collective-permute-start.11 = (bf16[1024,1024]{1,0:T(8,128)(2,1)}, bf16[1024,1024]{1,0:T(8,128)(2,1)}, u32[]{:S(2)}, u32[]{:S(2)}) collective-permute-start(bf16[1024,1024]{1,0:T(8,128)(2,1)} %refs_9_.3), channel_id=1, source_target_pairs={{0,1},{1,0},{2,3},{3,2},{4,5},{5,4},{6,7},{7,6},{8,9},{9,8},{10,11... | collective-permute-start | bytes 6291464 | tf_op jit(solution)/shard_map/ppermute | solution.py:843
  2.9 7.6 %collective-permute-start = (f32[8,1024]{1,0:T(8,128)S(1)}, f32[8,1024]{1,0:T(8,128)S(1)}, u32[]{:S(2)}, u32[]{:S(2)}) collective-permute-start(f32[8,1024]{1,0:T(8,128)S(1)} %dynamic_update_slice.3.refs_0_), channel_id=1, source_target_pairs={{0,1},{1,0},{2,3},{3,2},{4,5},{5,4},{6,7},{7,6},{8,9},{9,8},{10,11... | collective-permute-start | bytes 98312 | tf_op jit(solution)/shard_map/ppermute | solution.py:843
  5.4 13.5 %collective-permute-start.4 = (bf16[1,128,768]{2,1,0:T(8,128)(2,1)S(1)}, bf16[1,128,768]{2,1,0:T(8,128)(2,1)S(1)}, u32[]{:S(2)}, u32[]{:S(2)}) collective-permute-start(bf16[1,128,768]{2,1,0:T(8,128)(2,1)S(1)} %maximum_bitcast_fusion.refs_1_), channel_id=1, source_target_pairs={{0,16},{4,20},{8,24},{12,28},{16,0},{20,4},{24,8},{28,12},{1,17},{... | collective-permute-start | bytes 589832 | tf_op jit(solution)/shard_map/ppermute | solution.py:843
  9.1 17.2 %collective-permute-start.6 = (bf16[2,64,1024]{2,1,0:T(8,128)(2,1)}, bf16[2,64,1024]{2,1,0:T(8,128)(2,1)S(1)}, u32[]{:S(2)}, u32[]{:S(2)}) collective-permute-start(bf16[2,64,1024]{2,1,0:T(8,128)(2,1)} %refs_2_.1), channel_id=1, source_target_pairs={{0,2},{1,3},{2,0},{3,1},{4,6},{5,7},{6,4},{7,5},{8,10},{9,11},{10,... | collective-permute-start | bytes 786440 | tf_op jit(solution)/shard_map/ppermute | solution.py:843
  19.5 12.2 %collective-permute-start.5 = (bf16[2,128,768]{2,1,0:T(8,128)(2,1)S(1)}, bf16[2,128,768]{2,1,0:T(8,128)(2,1)S(1)}, u32[]{:S(2)}, u32[]{:S(2)}) collective-permute-start(bf16[2,128,768]{2,1,0:T(8,128)(2,1)S(1)} %bitcast.87), channel_id=1, source_target_pairs={{0,8},{4,12},{8,0},{12,4},{16,24},{20,28},{24,16},{28,20},{1,9},{5... | collective-permute-start | bytes 1179656 | tf_op jit(solution)/shard_map/ppermute | solution.py:843
  26.2 6.1 %collective-permute-start.3 = (f32[8,256]{1,0:T(8,128)S(1)}, f32[8,256]{1,0:T(8,128)S(1)}, u32[]{:S(2)}, u32[]{:S(2)}) collective-permute-start(f32[8,256]{1,0:T(8,128)S(1)} %pad_maximum_fusion.2), channel_id=1, source_target_pairs={{0,1},{1,0},{2,3},{3,2},{4,5},{5,4},{6,7},{7,6},{8,9},{9,8},{10,11... | collective-permute-start | bytes 24584 | tf_op jit(solution)/shard_map/ppermute | solution.py:843
  26.8 4.9 %collective-permute-start.8 = (f32[8,1024]{1,0:T(8,128)S(1)}, f32[8,1024]{1,0:T(8,128)S(1)}, u32[]{:S(2)}, u32[]{:S(2)}) collective-permute-start(f32[8,1024]{1,0:T(8,128)S(1)} %shard_map.404.refs_0_), channel_id=1, source_target_pairs={{0,16},{4,20},{8,24},{12,28},{16,0},{20,4},{24,8},{28,12},{1,17},{... | collective-permute-start | bytes 98312 | tf_op jit(solution)/shard_map/ppermute | solution.py:843
  32.3 11.6 %collective-permute-start.13 = (bf16[1024,768]{1,0:T(8,128)(2,1)S(1)}, bf16[1024,768]{1,0:T(8,128)(2,1)S(1)}, u32[]{:S(2)}, u32[]{:S(2)}) collective-permute-start(bf16[1024,768]{1,0:T(8,128)(2,1)S(1)} %pad_maximum_fusion.refs_7_.refs_8_), channel_id=1, source_target_pairs={{0,1},{1,0},{2,3},{3,2},{4,5},{5,4},{6,7},{7,6},{8,9},{9,8},{10,11... | collective-permute-start | bytes 4718600 | tf_op jit(solution)/shard_map/ppermute | solution.py:843
  32.9 27.8 %collective-permute-start.16 = (bf16[4,128,768]{2,1,0:T(8,128)(2,1)S(1)}, bf16[4,128,768]{2,1,0:T(8,128)(2,1)S(1)}, u32[]{:S(2)}, u32[]{:S(2)}) collective-permute-start(bf16[4,128,768]{2,1,0:T(8,128)(2,1)S(1)} %bitcast.79), channel_id=1, source_target_pairs={{0,4},{4,0},{8,12},{12,8},{16,20},{20,16},{24,28},{28,24},{1,5},{5... | collective-permute-start | bytes 2359304 | tf_op jit(solution)/shard_map/ppermute | solution.py:843
  42.3 14.2 %collective-permute-start.12 = (bf16[256,1024]{1,0:T(8,128)(2,1)S(1)}, bf16[256,1024]{1,0:T(8,128)(2,1)S(1)}, u32[]{:S(2)}, u32[]{:S(2)}) collective-permute-start(bf16[256,1024]{1,0:T(8,128)(2,1)S(1)} %get-tuple-element.325.refs_3_), channel_id=1, source_target_pairs={{0,2},{1,3},{2,0},{3,1},{4,6},{5,7},{6,4},{7,5},{8,10},{9,11},{10,... | collective-permute-start | bytes 1572872 | tf_op jit(solution)/shard_map/ppermute | solution.py:843
  61.4 14.9 %collective-permute-start.19 = (bf16[1024,768]{1,0:T(8,128)(2,1)S(1)}, bf16[1024,768]{1,0:T(8,128)(2,1)S(1)}, u32[]{:S(2)}, u32[]{:S(2)}) collective-permute-start(bf16[1024,768]{1,0:T(8,128)(2,1)S(1)} %bitcast.73), channel_id=1, source_target_pairs={{0,1},{1,0},{2,3},{3,2},{4,5},{5,4},{6,7},{7,6},{8,9},{9,8},{10,11... | collective-permute-start | bytes 4718600 | tf_op jit(solution)/shard_map/ppermute | solution.py:843
  62.1 14.3 %collective-permute-start.15 = (bf16[256,1024]{1,0:T(8,128)(2,1)S(1)}, bf16[256,1024]{1,0:T(8,128)(2,1)S(1)}, u32[]{:S(2)}, u32[]{:S(2)}) collective-permute-start(bf16[256,1024]{1,0:T(8,128)(2,1)S(1)} %get-tuple-element.330.refs_1_), channel_id=1, source_target_pairs={{0,2},{1,3},{2,0},{3,1},{4,6},{5,7},{6,4},{7,5},{8,10},{9,11},{10,... | collective-permute-start | bytes 1572872 | tf_op jit(solution)/shard_map/ppermute | solution.py:843
  79.9 27.2 %collective-permute-start.26 = (bf16[1024,1024]{1,0:T(8,128)(2,1)S(1)}, bf16[1024,1024]{1,0:T(8,128)(2,1)S(1)}, u32[]{:S(2)}, u32[]{:S(2)}) collective-permute-start(bf16[1024,1024]{1,0:T(8,128)(2,1)S(1)} %copy-done.9), channel_id=1, source_target_pairs={{0,1},{1,0},{2,3},{3,2},{4,5},{5,4},{6,7},{7,6},{8,9},{9,8},{10,11... | collective-permute-start | bytes 6291464 | tf_op jit(solution)/shard_map/ppermute | solution.py:843
  80.0 27.1 %collective-permute-start.27 = (bf16[1024,1024]{1,0:T(8,128)(2,1)S(1)}, bf16[1024,1024]{1,0:T(8,128)(2,1)S(1)}, u32[]{:S(2)}, u32[]{:S(2)}) collective-permute-start(bf16[1024,1024]{1,0:T(8,128)(2,1)S(1)} %copy-done.10), channel_id=1, source_target_pairs={{0,1},{1,0},{2,3},{3,2},{4,5},{5,4},{6,7},{7,6},{8,9},{9,8},{10,11... | collective-permute-start | bytes 6291464 | tf_op jit(solution)/shard_map/ppermute | solution.py:843
  80.5 11.0 %collective-permute-start.23 = (bf16[2,64,1024]{2,1,0:T(8,128)(2,1)S(1)}, bf16[2,64,1024]{2,1,0:T(8,128)(2,1)S(1)}, u32[]{:S(2)}, u32[]{:S(2)}) collective-permute-start(bf16[2,64,1024]{2,1,0:T(8,128)(2,1)S(1)} %copy-done.2), channel_id=1, source_target_pairs={{0,2},{1,3},{2,0},{3,1},{4,6},{5,7},{6,4},{7,5},{8,10},{9,11},{10,... | collective-permute-start | bytes 786440 | tf_op jit(solution)/shard_map/ppermute | solution.py:843
  96.1 11.0 %collective-permute-start.24 = (bf16[256,1024]{1,0:T(8,128)(2,1)S(1)}, bf16[256,1024]{1,0:T(8,128)(2,1)S(1)}, u32[]{:S(2)}, u32[]{:S(2)}) collective-permute-start(bf16[256,1024]{1,0:T(8,128)(2,1)S(1)} %get-tuple-element.348.refs_0_), channel_id=1, source_target_pairs={{0,2},{1,3},{2,0},{3,1},{4,6},{5,7},{6,4},{7,5},{8,10},{9,11},{10,... | collective-permute-start | bytes 1572872 | tf_op jit(solution)/shard_map/ppermute | solution.py:843
  97.4 15.0 %collective-permute-start.33 = (bf16[256,1024]{1,0:T(8,128)(2,1)S(1)}, bf16[256,1024]{1,0:T(8,128)(2,1)S(1)}, u32[]{:S(2)}, u32[]{:S(2)}) collective-permute-start(bf16[256,1024]{1,0:T(8,128)(2,1)S(1)} %get-tuple-element.366.refs_9_), channel_id=1, source_target_pairs={{0,1},{1,0},{2,3},{3,2},{4,5},{5,4},{6,7},{7,6},{8,9},{9,8},{10,11... | collective-permute-start | bytes 1572872 | tf_op jit(solution)/shard_map/ppermute | solution.py:843
  98.9 13.2 %collective-permute-start.34 = (bf16[256,256]{1,0:T(8,128)(2,1)S(1)}, bf16[256,256]{1,0:T(8,128)(2,1)S(1)}, u32[]{:S(2)}, u32[]{:S(2)}) collective-permute-start(bf16[256,256]{1,0:T(8,128)(2,1)S(1)} %get-tuple-element.367), channel_id=1, source_target_pairs={{0,1},{1,0},{2,3},{3,2},{4,5},{5,4},{6,7},{7,6},{8,9},{9,8},{10,11... | collective-permute-start | bytes 393224 | tf_op jit(solution)/shard_map/ppermute | solution.py:843
  112.1 14.3 %collective-permute-start.28 = (bf16[256,1024]{1,0:T(8,128)(2,1)S(1)}, bf16[256,1024]{1,0:T(8,128)(2,1)S(1)}, u32[]{:S(2)}, u32[]{:S(2)}) collective-permute-start(bf16[256,1024]{1,0:T(8,128)(2,1)S(1)} %get-tuple-element.356.refs_1_), channel_id=1, source_target_pairs={{0,2},{1,3},{2,0},{3,1},{4,6},{5,7},{6,4},{7,5},{8,10},{9,11},{10,... | collective-permute-start | bytes 1572872 | tf_op jit(solution)/shard_map/ppermute | solution.py:843
  132.5 13.9 %collective-permute-start.37 = (bf16[256,1024]{1,0:T(8,128)(2,1)S(1)}, bf16[256,1024]{1,0:T(8,128)(2,1)S(1)}, u32[]{:S(2)}, u32[]{:S(2)}) collective-permute-start(bf16[256,1024]{1,0:T(8,128)(2,1)S(1)} %get-tuple-element.382.refs_0_), channel_id=1, source_target_pairs={{0,2},{1,3},{2,0},{3,1},{4,6},{5,7},{6,4},{7,5},{8,10},{9,11},{10,... | collective-permute-start | bytes 1572872 | tf_op jit(solution)/shard_map/ppermute | solution.py:843
  148.7 13.1 %collective-permute-start.42 = (bf16[256,1024]{1,0:T(8,128)(2,1)S(1)}, bf16[256,1024]{1,0:T(8,128)(2,1)S(1)}, u32[]{:S(2)}, u32[]{:S(2)}) collective-permute-start(bf16[256,1024]{1,0:T(8,128)(2,1)S(1)} %get-tuple-element.392.refs_10_.refs_5_), channel_id=1, source_target_pairs={{0,1},{1,0},{2,3},{3,2},{4,5},{5,4},{6,7},{7,6},{8,9},{9,8},{10,11... | collective-permute-start | bytes 1572872 | tf_op jit(solution)/shard_map/ppermute | solution.py:843
  148.7 13.0 %collective-permute-start.41 = (bf16[64,1024]{1,0:T(8,128)(2,1)S(1)}, bf16[64,1024]{1,0:T(8,128)(2,1)S(1)}, u32[]{:S(2)}, u32[]{:S(2)}) collective-permute-start(bf16[64,1024]{1,0:T(8,128)(2,1)S(1)} %get-tuple-element.391), channel_id=1, source_target_pairs={{0,1},{1,0},{2,3},{3,2},{4,5},{5,4},{6,7},{7,6},{8,9},{9,8},{10,11... | collective-permute-start | bytes 393224 | tf_op jit(solution)/shard_map/ppermute | solution.py:843
  156.7 5.0 %collective-permute-start.40 = (f32[8,512]{1,0:T(8,128)S(1)}, f32[8,512]{1,0:T(8,128)S(1)}, u32[]{:S(2)}, u32[]{:S(2)}) collective-permute-start(f32[8,512]{1,0:T(8,128)S(1)} %shard_map.421.refs_1_), channel_id=1, source_target_pairs={{0,16},{4,20},{8,24},{12,28},{16,0},{20,4},{24,8},{28,12},{1,17},{... | collective-permute-start | bytes 49160 | tf_op jit(solution)/shard_map/ppermute | solution.py:843
  158.5 22.6 %collective-permute-start.47 = (bf16[4,128,1024]{2,1,0:T(8,128)(2,1)S(1)}, bf16[4,128,1024]{2,1,0:T(8,128)(2,1)S(1)}, u32[]{:S(2)}, u32[]{:S(2)}) collective-permute-start(bf16[4,128,1024]{2,1,0:T(8,128)(2,1)S(1)} %get-tuple-element.418), channel_id=1, source_target_pairs={{0,4},{4,0},{8,12},{12,8},{16,20},{20,16},{24,28},{28,24},{1,5},{5... | collective-permute-start | bytes 3145736 | tf_op jit(solution)/shard_map/ppermute | solution.py:843
  160.0 22.5 %collective-permute-start.46 = (bf16[4,128,1024]{2,1,0:T(8,128)(2,1)S(1)}, bf16[4,128,1024]{2,1,0:T(8,128)(2,1)S(1)}, u32[]{:S(2)}, u32[]{:S(2)}) collective-permute-start(bf16[4,128,1024]{2,1,0:T(8,128)(2,1)S(1)} %get-tuple-element.416), channel_id=1, source_target_pairs={{0,8},{4,12},{8,0},{12,4},{16,24},{20,28},{24,16},{28,20},{1,9},{5... | collective-permute-start | bytes 3145736 | tf_op jit(solution)/shard_map/ppermute | solution.py:843
  164.4 10.8 %collective-permute-start.43 = (bf16[256,1024]{1,0:T(8,128)(2,1)S(1)}, bf16[256,1024]{1,0:T(8,128)(2,1)S(1)}, u32[]{:S(2)}, u32[]{:S(2)}) collective-permute-start(bf16[256,1024]{1,0:T(8,128)(2,1)S(1)} %get-tuple-element.398.refs_0_), channel_id=1, source_target_pairs={{0,2},{1,3},{2,0},{3,1},{4,6},{5,7},{6,4},{7,5},{8,10},{9,11},{10,... | collective-permute-start | bytes 1572872 | tf_op jit(solution)/shard_map/ppermute | solution.py:843
  186.6 43.0 %collective-permute-start.55 = (bf16[4,128,1792]{2,1,0:T(8,128)(2,1)S(1)}, bf16[4,128,1792]{2,1,0:T(8,128)(2,1)S(1)}, u32[]{:S(2)}, u32[]{:S(2)}) collective-permute-start(bf16[4,128,1792]{2,1,0:T(8,128)(2,1)S(1)} %get-tuple-element.473), channel_id=1, source_target_pairs={{0,4},{4,0},{8,12},{12,8},{16,20},{20,16},{24,28},{28,24},{1,5},{5... | collective-permute-start | bytes 5505032 | tf_op jit(solution)/shard_map/ppermute | solution.py:843
  187.5 12.6 %collective-permute-start.45 = (bf16[256,1024]{1,0:T(8,128)(2,1)S(1)}, bf16[256,1024]{1,0:T(8,128)(2,1)S(1)}, u32[]{:S(2)}, u32[]{:S(2)}) collective-permute-start(bf16[256,1024]{1,0:T(8,128)(2,1)S(1)} %get-tuple-element.405.refs_1_), channel_id=1, source_target_pairs={{0,2},{1,3},{2,0},{3,1},{4,6},{5,7},{6,4},{7,5},{8,10},{9,11},{10,... | collective-permute-start | bytes 1572872 | tf_op jit(solution)/shard_map/ppermute | solution.py:843
  187.8 22.4 %collective-permute-start.52 = (bf16[2,128,1024]{2,1,0:T(8,128)(2,1)S(1)}, bf16[2,128,1024]{2,1,0:T(8,128)(2,1)S(1)}, u32[]{:S(2)}, u32[]{:S(2)}) collective-permute-start(bf16[2,128,1024]{2,1,0:T(8,128)(2,1)S(1)} %get-tuple-element.445), channel_id=1, source_target_pairs={{0,8},{4,12},{8,0},{12,4},{16,24},{20,28},{24,16},{28,20},{1,9},{5... | collective-permute-start | bytes 1572872 | tf_op jit(solution)/shard_map/ppermute | solution.py:843
  189.5 24.2 %collective-permute-start.51 = (bf16[1,256,1024]{2,1,0:T(8,128)(2,1)S(1)}, bf16[1,256,1024]{2,1,0:T(8,128)(2,1)S(1)}, u32[]{:S(2)}, u32[]{:S(2)}) collective-permute-start(bf16[1,256,1024]{2,1,0:T(8,128)(2,1)S(1)} %get-tuple-element.443), channel_id=1, source_target_pairs={{0,16},{4,20},{8,24},{12,28},{16,0},{20,4},{24,8},{28,12},{1,17},{... | collective-permute-start | bytes 1572872 | tf_op jit(solution)/shard_map/ppermute | solution.py:843
  206.8 7.5 %collective-permute-start.53 = (bf16[256,1024]{1,0:T(8,128)(2,1)S(1)}, bf16[256,1024]{1,0:T(8,128)(2,1)S(1)}, u32[]{:S(2)}, u32[]{:S(2)}) collective-permute-start(bf16[256,1024]{1,0:T(8,128)(2,1)S(1)} %get-tuple-element.463), channel_id=1, source_target_pairs={{0,1},{1,0},{2,3},{3,2},{4,5},{5,4},{6,7},{7,6},{8,9},{9,8},{10,11... | collective-permute-start | bytes 1572872 | tf_op jit(solution)/shard_map/ppermute | solution.py:843
  206.9 10.2 %collective-permute-start.50 = (bf16[256,1024]{1,0:T(8,128)(2,1)S(1)}, bf16[256,1024]{1,0:T(8,128)(2,1)S(1)}, u32[]{:S(2)}, u32[]{:S(2)}) collective-permute-start(bf16[256,1024]{1,0:T(8,128)(2,1)S(1)} %get-tuple-element.439.refs_1_), channel_id=1, source_target_pairs={{0,1},{1,0},{2,3},{3,2},{4,5},{5,4},{6,7},{7,6},{8,9},{9,8},{10,11... | collective-permute-start | bytes 1572872 | tf_op jit(solution)/shard_map/ppermute | solution.py:843
  210.2 9.4 %collective-permute-start.56 = (bf16[128,1024]{1,0:T(8,128)(2,1)S(1)}, bf16[128,1024]{1,0:T(8,128)(2,1)S(1)}, u32[]{:S(2)}, u32[]{:S(2)}) collective-permute-start(bf16[128,1024]{1,0:T(8,128)(2,1)S(1)} %get-tuple-element.477), channel_id=1, source_target_pairs={{0,2},{1,3},{2,0},{3,1},{4,6},{5,7},{6,4},{7,5},{8,10},{9,11},{10,... | collective-permute-start | bytes 786440 | tf_op jit(solution)/shard_map/ppermute | solution.py:843
  216.5 38.7 %collective-permute-start.59 = (bf16[4,128,1024]{2,1,0:T(8,128)(2,1)S(1)}, bf16[4,128,1024]{2,1,0:T(8,128)(2,1)S(1)}, u32[]{:S(2)}, u32[]{:S(2)}) collective-permute-start(bf16[4,128,1024]{2,1,0:T(8,128)(2,1)S(1)} %get-tuple-element.491), channel_id=1, source_target_pairs={{0,4},{4,0},{8,12},{12,8},{16,20},{20,16},{24,28},{28,24},{1,5},{5... | collective-permute-start | bytes 3145736 | tf_op jit(solution)/shard_map/ppermute | solution.py:843
  230.6 24.0 %collective-permute-start.60 = (bf16[2,128,1792]{2,1,0:T(8,128)(2,1)S(1)}, bf16[2,128,1792]{2,1,0:T(8,128)(2,1)S(1)}, u32[]{:S(2)}, u32[]{:S(2)}) collective-permute-start(bf16[2,128,1792]{2,1,0:T(8,128)(2,1)S(1)} %get-tuple-element.493), channel_id=1, source_target_pairs={{0,8},{4,12},{8,0},{12,4},{16,24},{20,28},{24,16},{28,20},{1,9},{5... | collective-permute-start | bytes 2752520 | tf_op jit(solution)/shard_map/ppermute | solution.py:843
  232.3 50.4 %collective-permute-start.54 = (bf16[4,128,1024]{2,1,0:T(8,128)(2,1)S(1)}, bf16[4,128,1024]{2,1,0:T(8,128)(2,1)S(1)}, u32[]{:S(2)}, u32[]{:S(2)}) collective-permute-start(bf16[4,128,1024]{2,1,0:T(8,128)(2,1)S(1)} %get-tuple-element.471), channel_id=1, source_target_pairs={{0,4},{4,0},{8,12},{12,8},{16,20},{20,16},{24,28},{28,24},{1,5},{5... | collective-permute-start | bytes 3145736 | tf_op jit(solution)/shard_map/ppermute | solution.py:843
  233.2 19.3 %collective-permute-start.61 = (bf16[1,128,1024]{2,1,0:T(8,128)(2,1)S(1)}, bf16[1,128,1024]{2,1,0:T(8,128)(2,1)S(1)}, u32[]{:S(2)}, u32[]{:S(2)}) collective-permute-start(bf16[1,128,1024]{2,1,0:T(8,128)(2,1)S(1)} %get-tuple-element.495), channel_id=1, source_target_pairs={{0,16},{4,20},{8,24},{12,28},{16,0},{20,4},{24,8},{28,12},{1,17},{... | collective-permute-start | bytes 786440 | tf_op jit(solution)/shard_map/ppermute | solution.py:843
  256.0 28.2 %collective-permute-start.66 = (bf16[2,128,1024]{2,1,0:T(8,128)(2,1)S(1)}, bf16[2,128,1024]{2,1,0:T(8,128)(2,1)S(1)}, u32[]{:S(2)}, u32[]{:S(2)}) collective-permute-start(bf16[2,128,1024]{2,1,0:T(8,128)(2,1)S(1)} %get-tuple-element.533), channel_id=1, source_target_pairs={{0,8},{4,12},{8,0},{12,4},{16,24},{20,28},{24,16},{28,20},{1,9},{5... | collective-permute-start | bytes 1572872 | tf_op jit(solution)/shard_map/ppermute | solution.py:843
  257.9 30.4 %collective-permute-start.65 = (bf16[1,128,1792]{2,1,0:T(8,128)(2,1)S(1)}, bf16[1,128,1792]{2,1,0:T(8,128)(2,1)S(1)}, u32[]{:S(2)}, u32[]{:S(2)}) collective-permute-start(bf16[1,128,1792]{2,1,0:T(8,128)(2,1)S(1)} %get-tuple-element.531), channel_id=1, source_target_pairs={{0,16},{4,20},{8,24},{12,28},{16,0},{20,4},{24,8},{28,12},{1,17},{... | collective-permute-start | bytes 1376264 | tf_op jit(solution)/shard_map/ppermute | solution.py:843
  264.1 13.5 %collective-permute-start.62 = (f32[8,1280]{1,0:T(8,128)S(1)}, f32[8,1280]{1,0:T(8,128)S(1)}, u32[]{:S(2)}, u32[]{:S(2)}) collective-permute-start(f32[8,1280]{1,0:T(8,128)S(1)} %shard_map.437.refs_0_), channel_id=1, source_target_pairs={{0,8},{4,12},{8,0},{12,4},{16,24},{20,28},{24,16},{28,20},{1,9},{5... | collective-permute-start | bytes 122888 | tf_op jit(solution)/shard_map/ppermute | solution.py:843
  277.6 5.1 %collective-permute-start.63 = (f32[8,1280]{1,0:T(8,128)S(1)}, f32[8,1280]{1,0:T(8,128)S(1)}, u32[]{:S(2)}, u32[]{:S(2)}) collective-permute-start(f32[8,1280]{1,0:T(8,128)S(1)} %shard_map.442.refs_0_), channel_id=1, source_target_pairs={{0,16},{4,20},{8,24},{12,28},{16,0},{20,4},{24,8},{28,12},{1,17},{... | collective-permute-start | bytes 122888 | tf_op jit(solution)/shard_map/ppermute | solution.py:843
  278.7 15.4 %collective-permute-start.70 = (f32[64,1024]{1,0:T(8,128)}, f32[64,1024]{1,0:T(8,128)}, u32[]{:S(2)}, u32[]{:S(2)}) collective-permute-start(f32[64,1024]{1,0:T(8,128)} %get-tuple-element.566), channel_id=1, source_target_pairs={{0,1},{1,0},{2,3},{3,2},{4,5},{5,4},{6,7},{7,6},{8,9},{9,8},{10,11... | collective-permute-start | bytes 786440 | tf_op jit(solution)/shard_map/ppermute | solution.py:843
  285.5 14.5 %collective-permute-start.68 = (bf16[1,128,1024]{2,1,0:T(8,128)(2,1)}, bf16[1,128,1024]{2,1,0:T(8,128)(2,1)}, u32[]{:S(2)}, u32[]{:S(2)}) collective-permute-start(bf16[1,128,1024]{2,1,0:T(8,128)(2,1)} %get-tuple-element.552), channel_id=1, source_target_pairs={{0,16},{4,20},{8,24},{12,28},{16,0},{20,4},{24,8},{28,12},{1,17},{... | collective-permute-start | bytes 786440 | tf_op jit(solution)/shard_map/ppermute | solution.py:843
  286.4 17.3 %collective-permute-start.64 = (bf16[2,128,1024]{2,1,0:T(8,128)(2,1)}, bf16[2,128,1024]{2,1,0:T(8,128)(2,1)}, u32[]{:S(2)}, u32[]{:S(2)}) collective-permute-start(bf16[2,128,1024]{2,1,0:T(8,128)(2,1)} %get-tuple-element.528), channel_id=1, source_target_pairs={{0,8},{4,12},{8,0},{12,4},{16,24},{20,28},{24,16},{28,20},{1,9},{5... | collective-permute-start | bytes 1572872 | tf_op jit(solution)/shard_map/ppermute | solution.py:843
  289.1 11.9 %collective-permute-start.67 = (f32[8,1280]{1,0:T(8,128)S(1)}, f32[8,1280]{1,0:T(8,128)S(1)}, u32[]{:S(2)}, u32[]{:S(2)}) collective-permute-start(f32[8,1280]{1,0:T(8,128)S(1)} %shard_map.443.refs_0_), channel_id=1, source_target_pairs={{0,4},{4,0},{8,12},{12,8},{16,20},{20,16},{24,28},{28,24},{1,5},{5... | collective-permute-start | bytes 122888 | tf_op jit(solution)/shard_map/ppermute | solution.py:843
  293.2 13.0 %collective-permute-start.71 = (bf16[1,128,1024]{2,1,0:T(8,128)(2,1)}, bf16[1,128,1024]{2,1,0:T(8,128)(2,1)S(1)}, u32[]{:S(2)}, u32[]{:S(2)}) collective-permute-start(bf16[1,128,1024]{2,1,0:T(8,128)(2,1)} %copy-done.7), channel_id=1, source_target_pairs={{0,4},{4,0},{8,12},{12,8},{16,20},{20,16},{24,28},{28,24},{1,5},{5... | collective-permute-start | bytes 786440 | tf_op jit(solution)/shard_map/ppermute | solution.py:843
  304.9 11.3 %collective-permute-start.69 = (bf16[1,128,1024]{2,1,0:T(8,128)(2,1)S(1)}, bf16[1,128,1024]{2,1,0:T(8,128)(2,1)S(1)}, u32[]{:S(2)}, u32[]{:S(2)}) collective-permute-start(bf16[1,128,1024]{2,1,0:T(8,128)(2,1)S(1)} %get-tuple-element.564), channel_id=1, source_target_pairs={{0,16},{4,20},{8,24},{12,28},{16,0},{20,4},{24,8},{28,12},{1,17},{... | collective-permute-start | bytes 786440 | tf_op jit(solution)/shard_map/ppermute | solution.py:843
  (44 other events, 246.7 us)
